TPU v7x, 32 devices: a whole 2x2x4 slice. The times are simulated.
32 devices in a mesh: seq: 8 (over z, y), head: 4 (over x, core).
Axes of the slice: x: 2, y: 2, z: 4, core: 2. Of those that a mesh axis runs over, the one named last changes fastest.
Arguments:
- tokens: bfloat16 [4096, 2048], P(('seq', 'head')), may hold values from -6 to 6
- w_in_x: bfloat16 [2048, 4096], P(None, 'head'), may hold values from -0.125 to 0.125
- w_in_z: bfloat16 [2048, 4096], P(None, 'head'), may hold values from -0.125 to 0.125
- w_in_bc: bfloat16 [2048, 256], replicated, may hold values from -0.125 to 0.125
- w_dt: bfloat16 [2048, 64], P(None, 'head'), may hold values from -0.125 to 0.125
- conv_x: float32 [4, 4096], P(None, 'head'), may hold values from -3 to 3
- conv_bc: float32 [4, 256], replicated, may hold values from -3 to 3
- dt_bias: float32 [64], P('head'), may hold values from -1 to 1
- decay_rate: float32 [64], P('head'), may hold values from 1.2207031e-05 to 0.05, as said below
- skip: float32 [64], P('head'), may hold values from 0.5 to 1.5
- norm_gain: float32 [4096], P('head'), may hold values from 0.25 to 1.75
- w_out: bfloat16 [4096, 2048], P('head'), may hold values from -0.09375 to 0.09375
Outputs:
- mixed: bfloat16 [4096, 2048], P(('seq', 'head'))
Inputs may be any that keep to these rules, and one draw needn't show every extreme that they name: `decay_rate`: positive per-head decay rates.
All inputs are finite; a program needn't handle non-finite values.
Results may differ from a plain program's by a relative error of at most 0.013.
Values may be sent and summed in bfloat16 or wider, within the bound.
A program may use at most 128 MiB of HBM per device.

v0:
```python
import jax
import jax.numpy as jnp
from jax import lax
from jax.sharding import PartitionSpec as P

SPAN = 256
KERNEL = 4
E = 4096


highest = lax.Precision.HIGHEST


def passed_along(block, axis, distance):
    devices = range(lax.axis_size(axis))
    route = [(i - distance, i) for i in devices if i - distance in devices]
    return lax.ppermute(block, axis, route)


def carried_in(shard, axis, combine, identity):
    size, index = (lax.axis_size(axis), lax.axis_index(axis))
    everything = jax.tree.map(lambda part: lax.all_gather(part, axis), shard)
    start = jax.tree.map(
        lambda part, zero: jnp.broadcast_to(jnp.asarray(zero, part.dtype), part.shape),
        shard,
        identity,
    )

    def step(k, before):
        reached = k < index
        new = combine(before, jax.tree.map(lambda part: part[k], everything))
        return jax.tree.map(lambda a, b: jnp.where(reached, a, b), new, before)

    return lax.fori_loop(0, size, step, start)


def span_update(state, x_span, step_span, decay_span, b_span, c_span, skip):
    cumul = jnp.cumsum(decay_span, axis=0)
    length = x_span.shape[0]
    lower = jnp.arange(length)[:, None] >= jnp.arange(length)[None, :]
    spread = cumul.T[:, :, None] - cumul.T[:, None, :]
    within = jnp.exp(jnp.where(lower[None], spread, -jnp.inf))
    scores = jnp.dot(c_span, b_span.T, precision=highest)
    scaled = x_span * step_span[:, :, None]
    output = jnp.einsum("hts,shp->thp", within * scores[None], scaled, precision=highest)
    output = (
        output
        + jnp.einsum("tn,hpn->thp", c_span, state, precision=highest) * jnp.exp(cumul)[:, :, None]
    )
    output = output + skip[None, :, None] * x_span
    remain = jnp.exp(cumul[-1][None, :] - cumul)
    fresh = jnp.einsum("shp,sn->hpn", scaled * remain[:, :, None], b_span, precision=highest)
    return (jnp.exp(cumul[-1])[:, None, None] * state + fresh, output, cumul)


def causal_conv(values, before, kernel):
    padded = jnp.concatenate([before, values], axis=0)
    length = values.shape[0]
    result = kernel[0] * padded[0:length]
    for offset in range(1, kernel.shape[0]):
        result = result + kernel[offset] * padded[offset : offset + length]
    return jax.nn.silu(result)


def per_device(
    tokens,
    w_in_x,
    w_in_z,
    w_in_bc,
    w_dt,
    conv_x,
    conv_bc,
    dt_bias,
    decay_rate,
    skip,
    norm_gain,
    w_out,
):
    inner_cols = w_in_x.shape[1]
    head_count = dt_bias.shape[0]
    head_width = inner_cols // head_count
    state_size = w_in_bc.shape[1] // 2
    block_rows = lax.all_gather(tokens, "head", axis=0, tiled=True)
    joined = jnp.concatenate(
        [
            jnp.dot(block_rows, w_in_x, preferred_element_type=jnp.float32),
            jnp.dot(block_rows, w_in_z, preferred_element_type=jnp.float32),
            jnp.dot(block_rows, w_in_bc, preferred_element_type=jnp.float32),
            jnp.dot(block_rows, w_dt, preferred_element_type=jnp.float32),
        ],
        axis=1,
    )
    x_proj = joined[:, :inner_cols]
    gate_proj = joined[:, inner_cols : 2 * inner_cols]
    bc_proj = joined[:, 2 * inner_cols : 2 * inner_cols + 2 * state_size]
    step_raw = joined[:, 2 * inner_cols + 2 * state_size :]
    margin = KERNEL - 1
    x_before, bc_before = passed_along((x_proj[-margin:], bc_proj[-margin:]), "seq", 1)
    x_conv = causal_conv(x_proj, x_before, conv_x)
    bc_conv = causal_conv(bc_proj, bc_before, conv_bc)
    step_size = jax.nn.softplus(step_raw + dt_bias)
    log_decay = -step_size * decay_rate
    seg_rows = x_proj.shape[0]
    spans = seg_rows // SPAN

    def advance(carry, inputs):
        state, offset = carry
        x_span, step_span, decay_span, bc_span = inputs
        state, output, cumul = span_update(
            state,
            x_span,
            step_span,
            decay_span,
            bc_span[:, :state_size],
            bc_span[:, state_size:],
            skip,
        )
        return ((state, offset + cumul[-1]), (output, cumul + offset))

    empty_state = jnp.zeros((head_count, head_width, state_size), jnp.float32)
    empty_decay = jnp.zeros((head_count,), jnp.float32)
    (final_state, totals), (outputs, cumuls) = lax.scan(
        advance,
        (empty_state, empty_decay),
        (
            x_conv.reshape(spans, SPAN, head_count, head_width),
            step_size.reshape(spans, SPAN, head_count),
            log_decay.reshape(spans, SPAN, head_count),
            bc_conv.reshape(spans, SPAN, 2 * state_size),
        ),
    )
    local_out = outputs.reshape(seg_rows, head_count, head_width)
    segment_cumul = cumuls.reshape(seg_rows, head_count)

    def combine(earlier, later):
        return (earlier[0] + later[0], jnp.exp(later[0])[:, None, None] * earlier[1] + later[1])

    entering = carried_in((totals, final_state), "seq", combine, (empty_decay, empty_state))[1]
    c_matrix = bc_conv[:, state_size:]
    carried = (
        jnp.einsum("tn,hpn->thp", c_matrix, entering, precision=highest)
        * jnp.exp(segment_cumul)[:, :, None]
    )
    ssd_out = (local_out + carried).reshape(seg_rows, inner_cols)
    gated = ssd_out * jax.nn.silu(gate_proj)
    squares = lax.psum(jnp.sum(gated * gated, axis=1), "head")
    normed = (gated * lax.rsqrt(squares / E + 1e-05)[:, None] * norm_gain).astype(jnp.bfloat16)
    result = lax.psum_scatter(
        jnp.dot(normed, w_out, preferred_element_type=jnp.float32).astype(jnp.bfloat16),
        "head",
        scatter_dimension=0,
        tiled=True,
    )
    return result


def solution(mesh):
    placed = (
        P(("seq", "head"), None),
        P(None, "head"),
        P(None, "head"),
        P(),
        P(None, "head"),
        P(None, "head"),
        P(),
        P("head"),
        P("head"),
        P("head"),
        P("head"),
        P("head", None),
    )
    return jax.shard_map(
        per_device, mesh=mesh, in_specs=placed, out_specs=P(("seq", "head"), None), check_vma=False
    )
```

profile of v0, /device:TPU:28, one launch (start us, length us, event | category | flops | bytes accessed | tf_op | source)
XLA Modules:
  0.0 283.3 jit_solution(1241037299867360052)
XLA Ops:
  6.5 0.7 all-gather.5.cloned.1.call-update
  7.3 0.8 fusion.58
  8.2 0.9 fusion.57
  9.1 23.3 %all-gather.5.cloned.1.call-done = bf16[512,2048]{1,0:T(8,128)(2,1)} async-done(((bf16[128,2048]{1,0:T(8,128)(2,1)}), bf16[512,2048]{1,0:T(8,128)(2,1)}) %all-gather.5.cloned.1.call-update) | async-done | bytes 2097168 | tf_op jit(solution)/shard_map/all_gather | solution.py:83
  32.4 2.4 fusion.60
  34.9 0.8 copy-done.7
  35.7 1.4 collective-permute-start.1
  37.1 4.5 %fusion.59 = f32[512,1024]{1,0:T(8,128)S(1)} fusion(bf16[512,2048]{1,0:T(8,128)(2,1)S(1)} %copy-done.5, bf16[2048,1024]{1,0:T(8,128)(2,1)} %param.17), kind=kOutput, calls=%fused_computation.97 | convolution fusion | flops 2147483648 | bytes 8388608 | tf_op jit(solution)/shard_map/dot_general | solution.py:86
  41.7 1.5 collective-permute-start
  43.2 0.7 negate_multiply_fusion
  44.0 2.8 divide_multiply_fusion.1
  46.8 1.2 collective-permute-done
  47.9 4.8 %divide_multiply_fusion = f32[512,1024]{1,0:T(8,128)S(1)} fusion(f32[512,1024]{1,0:T(8,128)} %copy-done.4, f32[3,1024]{1,0:T(4,128)S(1)} %collective-permute-done, f32[1024]{0:T(1024)S(1)} %bitcast.147, f32[1024]{0:T(1024)S(1)} %bitcast.148, f32[1024]{0:T(1024)S(1)} %bitcast.146, f32[1024]{0:T(1024)S(1)} %bitcast.145), kind=kLoop, calls=%fused_computation.73 | loop fusion | flops 7340032 | bytes 4222976 | tf_op jit(solution)/shard_map/jit(silu)/mul | solution.py:62
  52.7 2.5 reshape.110
  55.3 3.5 %copy.44 = f32[2,256,16,64]{1,3,2,0:T(8,128)S(1)} copy(f32[2,256,16,64]{3,2,1,0:T(8,128)} %reshape.110) | data formatting | bytes 4194304
  58.8 75.1 %while.31 = (s32[]{:T(128)}, f32[16,64,128]{2,1,0:T(8,128)}, f32[16]{0:T(128)S(1)}, f32[2,256,16,64]{1,0,3,2:T(2,128)}, f32[2,256,16]{1,2,0:T(8,128)}, /*index=5...) while((s32[]{:T(128)}, f32[16,64,128]{2,1,0:T(8,128)}, ...), condition=%wide.region_3.4_spmd.clone, body=%wide.region_0.3_spmd.clone.sunk | while | flops 1717387392 | bytes 31200088 | solution.py:122
  59.7 1.0 dynamic-slice_bitcast_fusion.2
  61.1 5.7 %fusion.92 = f32[256,16,64]{0,2,1:T(8,128)} fusion(f32[256,256]{1,0:T(8,128)S(1)} %fusion.91, f32[16,256]{1,0:T(8,128)S(1)} %get-tuple-element.403, pred[256,256]{1,0:T(8,128)(4,1)S(1)} %iota_compare_fusion.2, f32[2,256,16,64]{1,3,2,0:T(8,128)S(1)} %get-tuple-element.443, s32[]{:T(128)} %get-tuple-element.424, f32[256,16]{0,1:T(8,128)S(1)} %bitcast.141), kind=kOutput, calls=%fused_computation.13.clone.1 | convolution fusion | flops 808714240 | bytes 2473988 | tf_op jit(solution)/shard_map/while/body/eval_jaxpr/hts,shp->thp/dot_general | solution.py:45
  67.1 2.2 fusion.93
  69.4 1.1 copy.86
  70.5 21.9 %dynamic_update_slice.14 = f32[2,256,16,64]{1,0,3,2:T(2,128)} dynamic-update-slice(f32[2,256,16,64]{1,0,3,2:T(2,128)} %get-tuple-element.427, f32[1,256,16,64]{1,0,3,2:T(1,128)S(1)} %copy.86, s32[]{:T(128)} %get-tuple-element.424, s32[]{:T(128)} %constant.64.clone.1..sunk, s32[]{:T(128)} %constant.64.clone.1..sunk, s32[]{:T(128)} %constant.64.clone.1..sunk) | dynamic-update-slice | bytes 2097156 | tf_op jit(solution)/shard_map/while/body/jit(dynamic_update_index_in_dim)/dynamic_update_slice | solution.py:122
  92.4 3.2 %convolution_add_fusion.3 = f32[16,64,128]{2,1,0:T(8,128)} fusion(f32[2,256,16,64]{1,3,2,0:T(8,128)} %copy-done.1, s32[]{:T(128)} %get-tuple-element.424, f32[256,16]{0,1:T(8,128)S(1)} %get-tuple-element.399, f32[256,16]{0,1:T(8,128)S(1)} %bitcast.142, f32[16,64,128]{2,1,0:T(8,128)} %get-tuple-element.425, f32[16]{0:T(128)S(1)} %get-tuple-element.401, ...), kind=kOutput, calls=%fused_computation.18.clone.1 | convolution fusion | flops 403570688 | bytes 2262017 | tf_op jit(solution)/shard_map/while/body/eval_jaxpr/shp,sn->hpn/dot_general | solution.py:52
  95.6 0.6 copy-done.10
  97.1 1.0 dynamic-slice_bitcast_fusion.2
  98.5 5.7 %fusion.92 = f32[256,16,64]{0,2,1:T(8,128)} fusion(f32[256,256]{1,0:T(8,128)S(1)} %fusion.91, f32[16,256]{1,0:T(8,128)S(1)} %get-tuple-element.403, pred[256,256]{1,0:T(8,128)(4,1)S(1)} %iota_compare_fusion.2, f32[2,256,16,64]{1,3,2,0:T(8,128)S(1)} %get-tuple-element.443, s32[]{:T(128)} %get-tuple-element.424, f32[256,16]{0,1:T(8,128)S(1)} %bitcast.141), kind=kOutput, calls=%fused_computation.13.clone.1 | convolution fusion | flops 808714240 | bytes 2473988 | tf_op jit(solution)/shard_map/while/body/eval_jaxpr/hts,shp->thp/dot_general | solution.py:45
  104.5 2.4 fusion.93
  107.0 1.1 copy.86
  108.0 21.9 %dynamic_update_slice.14 = f32[2,256,16,64]{1,0,3,2:T(2,128)} dynamic-update-slice(f32[2,256,16,64]{1,0,3,2:T(2,128)} %get-tuple-element.427, f32[1,256,16,64]{1,0,3,2:T(1,128)S(1)} %copy.86, s32[]{:T(128)} %get-tuple-element.424, s32[]{:T(128)} %constant.64.clone.1..sunk, s32[]{:T(128)} %constant.64.clone.1..sunk, s32[]{:T(128)} %constant.64.clone.1..sunk) | dynamic-update-slice | bytes 2097156 | tf_op jit(solution)/shard_map/while/body/jit(dynamic_update_index_in_dim)/dynamic_update_slice | solution.py:122
  129.9 3.3 %convolution_add_fusion.3 = f32[16,64,128]{2,1,0:T(8,128)} fusion(f32[2,256,16,64]{1,3,2,0:T(8,128)} %copy-done.1, s32[]{:T(128)} %get-tuple-element.424, f32[256,16]{0,1:T(8,128)S(1)} %get-tuple-element.399, f32[256,16]{0,1:T(8,128)S(1)} %bitcast.142, f32[16,64,128]{2,1,0:T(8,128)} %get-tuple-element.425, f32[16]{0:T(128)S(1)} %get-tuple-element.401, ...), kind=kOutput, calls=%fused_computation.18.clone.1 | convolution fusion | flops 403570688 | bytes 2262017 | tf_op jit(solution)/shard_map/while/body/eval_jaxpr/shp,sn->hpn/dot_general | solution.py:52
  134.0 1.3 dynamic-slice
  136.3 18.6 %all-reduce = f32[128]{0:T(128)S(1)} all-reduce(f32[128]{0:T(128)S(1)} %dynamic-update-slice), channel_id=2, replica_groups=mesh['seq'=8,'head'=4] {'seq'}, use_global_device_ids=true, to_apply=%add | all-reduce | flops 128 | bytes 1024
  154.9 3.9 %reshape.96 = f32[512,16,64]{0,2,1:T(8,128)} reshape(f32[2,256,16,64]{1,0,3,2:T(2,128)} %get-tuple-element.154) | data formatting | bytes 4194304 | tf_op jit(solution)/shard_map/reshape | solution.py:132
  158.9 47.9 %all-gather.7.cloned.1.call-done = f32[128,64,128]{2,1,0:T(8,128)} async-done(((f32[16,64,128]{2,1,0:T(8,128)}), f32[128,64,128]{2,1,0:T(8,128)}) %all-gather.7.cloned.1.call-update) | async-done | bytes 4194320 | tf_op jit(solution)/shard_map/all_gather | solution.py:22
  206.8 9.7 %while.32 = (s32[]{:T(128)}, f32[16,64,128]{2,1,0:T(8,128)S(1)}, s32[]{:T(128)}, f32[8,16]{1,0:T(8,128)S(1)}, f32[8,16,64,128]{3,2,1,0:T(8,128)}, /*index=5*/s32[]{:T(128)}, s32[]{:T(128)}) while((s32[]{:T(128)}, f32[16,64,128]{2,1,0:T(8,128)S(1)}, s32[]{:T(128)}, f32[8,16]{1,0:T(8,128)S(1)}, f32[8,16,64,128]{3,2,1,0:T(8,128)}, ...), condition=%wide.region_5.6_spmd.clone, body=%wide.region_4.5_spmd.clone.sunk | while | flops 524292 | bytes 1573161 | solution.py:34
  206.8 1.2 fusion.94
  208.1 1.2 fusion.94
  209.3 1.2 fusion.94
  210.5 1.2 fusion.94
  211.7 1.2 fusion.94
  212.9 1.2 fusion.94
  214.1 1.2 fusion.94
  215.3 1.2 fusion.94
  216.5 4.8 %multiply_add_fusion = f32[512,16,64]{0,2,1:T(8,128)} fusion(f32[512,16,64]{0,2,1:T(8,128)} %reshape.96, f32[16,64,128]{2,1,0:T(8,128)S(1)} %get-tuple-element.157, f32[512,16]{0,1:T(8,128)S(1)} %bitcast.144, f32[512,256]{1,0:T(8,128)S(1)} %bitcast.139), kind=kOutput, calls=%fused_computation.72 | convolution fusion | flops 806354944 | bytes 5013504 | tf_op jit(solution)/shard_map/tn,hpn->thp/dot_general | solution.py:141
  221.3 3.1 %copy.48 = f32[512,1024]{1,0:T(8,128)} copy(f32[512,1024]{0,1:T(8,128)} %bitcast.140) | data formatting | bytes 4194304 | tf_op jit(solution)/shard_map/reshape | solution.py:144
  224.4 6.7 %multiply_reduce_fusion = (f32[512]{0:T(512)S(1)}, f32[512,1024]{1,0:T(8,128)}) fusion(f32[512,1024]{1,0:T(8,128)} %copy.48, bf16[512,2048]{1,0:T(8,128)(2,1)S(1)} %copy-done.6, bf16[2048,1024]{1,0:T(8,128)(2,1)} %param.18), kind=kOutput, calls=%fused_computation.70 | convolution fusion | flops 2151153152 | bytes 10487808 | tf_op jit(solution)/shard_map/dot_general | solution.py:87
  231.1 6.4 %psum.7 = f32[512]{0:T(512)S(1)} all-reduce(f32[512]{0:T(512)S(1)} %get-tuple-element.299), channel_id=1, replica_groups=mesh['seq'=8,'head'=4] {'head'}, use_global_device_ids=true, to_apply=%region_7.8 | all-reduce | flops 512 | bytes 4096 | tf_op jit(solution)/shard_map/psum | solution.py:146
  237.5 7.5 %convolution_convert_fusion = bf16[512,2048]{1,0:T(8,128)(2,1)} fusion(bf16[1024,2048]{1,0:T(8,128)(2,1)} %param.27, f32[1024]{0:T(1024)S(1)} %copy-done.15, f32[512]{0:T(512)S(1)} %add_rsqrt_fusion, f32[512,1024]{1,0:T(8,128)} %copy.48, f32[512,1024]{1,0:T(8,128)} %get-tuple-element.300), kind=kOutput, calls=%fused_computation.59 | convolution fusion | flops 2152726528 | bytes 10491904 | tf_op jit(solution)/shard_map/dot_general | solution.py:149
  245.1 31.7 %reduce-scatter.2.cloned.1.call-done = bf16[128,2048]{1,0:T(8,128)(2,1)} async-done(((bf16[512,2048]{1,0:T(8,128)(2,1)}), bf16[128,2048]{1,0:T(8,128)(2,1)}) %reduce-scatter.2.cloned.1.call-update) | async-done | bytes 524304 | tf_op jit(solution)/shard_map/reduce_scatter | solution.py:148
  (95 shorter events, 4.6 us)
Async XLA Ops:
  6.5 25.9 %copy-start = (bf16[2048,256]{1,0:T(8,128)(2,1)S(1)}, bf16[2048,256]{1,0:T(8,128)(2,1)}, u32[]{:S(2)}) copy-start(bf16[2048,256]{1,0:T(8,128)(2,1)} %param.19) | copy-start | bytes 3145732
  6.5 25.9 %all-gather.5.cloned.1.call-start = ((), (), s32[]{:S(2)}) async-start(), calls=%async_computation.1 | async-start | bytes 2621440 | tf_op jit(solution)/shard_map/all_gather | solution.py:83
  7.3 199.5 %all-gather.7.cloned.1.call-start = ((), (), s32[]{:S(2)}) async-start(), calls=%async_computation.3 | async-start | bytes 4718592 | tf_op jit(solution)/shard_map/all_gather | solution.py:22
  32.4 4.7 %copy-start.5 = (bf16[512,2048]{1,0:T(8,128)(2,1)S(1)}, bf16[512,2048]{1,0:T(8,128)(2,1)}, u32[]{:S(2)}) copy-start(bf16[512,2048]{1,0:T(8,128)(2,1)} %all-gather.5.cloned.1.call-done) | copy-start | bytes 6291460
  34.9 0.8 copy-start.7
  35.7 7.5 %copy-start.8 = (bf16[2048,16]{0,1:T(8,128)(2,1)S(1)}, bf16[2048,16]{0,1:T(8,128)(2,1)}, u32[]{:S(2)}) copy-start(bf16[2048,16]{0,1:T(8,128)(2,1)} %param.20) | copy-start | bytes 196612
  35.7 7.5 %copy-start.13 = (f32[16]{0:T(128)S(1)}, f32[16]{0:T(128)}, u32[]{:S(2)}) copy-start(f32[16]{0:T(128)} %param.24) | copy-start | bytes 196
  35.7 7.5 %copy-start.14 = (f32[16]{0:T(128)S(1)}, f32[16]{0:T(128)}, u32[]{:S(2)}) copy-start(f32[16]{0:T(128)} %param.23) | copy-start | bytes 196
  35.7 8.3 %collective-permute-start.1 = (f32[3,256]{1,0:T(4,128)S(1)}, f32[3,256]{1,0:T(4,128)S(1)}, u32[]{:S(2)}, u32[]{:S(2)}) collective-permute-start(f32[3,256]{1,0:T(4,128)S(1)} %slice.99), channel_id=1, source_target_pairs={{0,4},{4,8},{8,12},{12,16},{16,20},{20,24},{24,28},{1,5},{5,9},{9,... | collective-permute-start | bytes 9224 | tf_op jit(solution)/shard_map/ppermute | solution.py:17
  41.7 6.3 %copy-start.4 = (f32[512,1024]{1,0:T(8,128)}, f32[512,1024]{1,0:T(8,128)S(1)}, u32[]{:S(2)}) copy-start(f32[512,1024]{1,0:T(8,128)S(1)} %fusion.59) | copy-start | bytes 6291460
  41.7 6.3 %collective-permute-start = (f32[3,1024]{1,0:T(4,128)S(1)}, f32[3,1024]{1,0:T(4,128)S(1)}, u32[]{:S(2)}, u32[]{:S(2)}) collective-permute-start(f32[3,1024]{1,0:T(4,128)S(1)} %slice.94), channel_id=1, source_target_pairs={{0,4},{4,8},{8,12},{12,16},{16,20},{20,24},{24,28},{1,5},{5,9},{9,... | collective-permute-start | bytes 36872 | tf_op jit(solution)/shard_map/ppermute | solution.py:17
  55.3 3.5 %copy-start.12 = (f32[16]{0:T(128)S(1)}, f32[16]{0:T(128)}, u32[]{:S(2)}) copy-start(f32[16]{0:T(128)} %param.25) | copy-start | bytes 196
  58.8 8.3 %copy-start.1 = (f32[2,256,16,64]{1,3,2,0:T(8,128)}, f32[2,256,16,64]{1,3,2,0:T(8,128)S(1)}, u32[]{:S(2)}) copy-start(f32[2,256,16,64]{1,3,2,0:T(8,128)S(1)} %get-tuple-element.443) | copy-start | bytes 6291460 | tf_op jit(solution)/shard_map/while
  92.4 3.2 %copy-start.9 = (f32[2,256,16]{1,2,0:T(8,128)S(1)}, f32[2,256,16]{1,2,0:T(8,128)}, u32[]{:S(2)}) copy-start(f32[2,256,16]{1,2,0:T(8,128)} %get-tuple-element.428) | copy-start | bytes 98308 | tf_op jit(solution)/shard_map/while
  92.4 3.9 %copy-start.2 = (f32[2,256,16,64]{1,3,2,0:T(8,128)S(1)}, f32[2,256,16,64]{1,3,2,0:T(8,128)}, u32[]{:S(2)}) copy-start(f32[2,256,16,64]{1,3,2,0:T(8,128)} %copy-done.1) | copy-start | bytes 6291460 | tf_op jit(solution)/shard_map/while
  95.6 0.6 copy-start.10
  96.2 8.3 %copy-start.1 = (f32[2,256,16,64]{1,3,2,0:T(8,128)}, f32[2,256,16,64]{1,3,2,0:T(8,128)S(1)}, u32[]{:S(2)}) copy-start(f32[2,256,16,64]{1,3,2,0:T(8,128)S(1)} %get-tuple-element.443) | copy-start | bytes 6291460 | tf_op jit(solution)/shard_map/while
  129.9 3.3 %copy-start.9 = (f32[2,256,16]{1,2,0:T(8,128)S(1)}, f32[2,256,16]{1,2,0:T(8,128)}, u32[]{:S(2)}) copy-start(f32[2,256,16]{1,2,0:T(8,128)} %get-tuple-element.428) | copy-start | bytes 98308 | tf_op jit(solution)/shard_map/while
  129.9 4.0 %copy-start.2 = (f32[2,256,16,64]{1,3,2,0:T(8,128)S(1)}, f32[2,256,16,64]{1,3,2,0:T(8,128)}, u32[]{:S(2)}) copy-start(f32[2,256,16,64]{1,3,2,0:T(8,128)} %copy-done.1) | copy-start | bytes 6291460 | tf_op jit(solution)/shard_map/while
  133.3 0.6 copy-start.10
  133.9 142.8 %reduce-scatter.2.cloned.1.call-start = ((), (), s32[]{:S(2)}) async-start(), calls=%async_computation.2 | async-start | bytes 2621440 | tf_op jit(solution)/shard_map/reduce_scatter | solution.py:148
  154.9 3.9 %copy-start.11 = (f32[2,256,16]{1,2,0:T(8,128)S(1)}, f32[2,256,16]{1,2,0:T(8,128)}, u32[]{:S(2)}) copy-start(f32[2,256,16]{1,2,0:T(8,128)} %get-tuple-element.158) | copy-start | bytes 98308
  206.8 9.8 %copy-start.3 = (f32[2,256,256]{2,1,0:T(8,128)S(1)}, f32[2,256,256]{2,1,0:T(8,128)}, u32[]{:S(2)}) copy-start(f32[2,256,256]{2,1,0:T(8,128)} %get-tuple-element.476) | copy-start | bytes 1572868
  221.3 3.1 %copy-start.6 = (bf16[512,2048]{1,0:T(8,128)(2,1)S(1)}, bf16[512,2048]{1,0:T(8,128)(2,1)}, u32[]{:S(2)}) copy-start(bf16[512,2048]{1,0:T(8,128)(2,1)} %all-gather.5.cloned.1.call-done) | copy-start | bytes 6291460
  224.4 13.2 %copy-start.15 = (f32[1024]{0:T(1024)S(1)}, f32[1024]{0:T(1024)}, u32[]{:S(2)}) copy-start(f32[1024]{0:T(1024)} %param.26) | copy-start | bytes 12292
Sparse Core Ops, SparseCore 0:
  8.9 23.4 all-gather.4
  134.1 72.6 all-gather.6
  245.2 31.5 reduce-scatter.1
where the time goes:
time: 289 us; the launch traced here: 283 us
  waiting for transfers between devices  105 us (36%)
  local copies, waits for them, and re-layouts  67.2 us (23%)
  matrix products  50 us (17%)
  blocking collectives  25 us (9%)
  other arithmetic  18.9 us (7%)
  between operations  14 us (5%)
  starting transfers between devices  2.97 us (1%)
    all_gather x1, waiting for transfers between devices, carried_in(): everything = jax.tree.map(lambda part: lax.all_gather(part, axis), shard)  47.9 us
    dynamic_update_slice x4, local copies, waits for them, and re-layouts, per_device(): lax.scan(advance, (empty_state, empty_decay), (x_conv.reshape(spans, SPAN...  45.9 us
    reduce_scatter x1, waiting for transfers between devices, per_device(): lax.psum_scatter(jnp.dot(normed, w_out, preferred_element_type=jnp.float3...  31.7 us
    all_gather x1, waiting for transfers between devices, per_device(): block_rows = lax.all_gather(tokens, 'head', axis=0, tiled=True)  23.3 us
    unnamed x1, blocking collectives  18.6 us
    dot_general x2, matrix products, span_update(): jnp.einsum('hts,shp->thp', within * scores[None], scaled, precision=highest)  11.4 us
    select_n x8, other arithmetic, step(): return jax.tree.map(lambda a, b: jnp.where(reached, a, b), new, before)  9.44 us
    mul x2, other arithmetic, causal_conv(): return jax.nn.silu(result)  7.62 us
  transfers between devices with their start and end apart: 5, of which 4 were waited for; matrix products, arithmetic and copies ran while one was open for 5% of the time, Pallas kernels for 0%

commit v1 on v0

v1 whole, which is shorter than its diff:
```python
import functools
import jax
import jax.numpy as jnp
from jax import lax
from jax.experimental import pallas as pl
from jax.experimental.pallas import tpu as pltpu
from jax.sharding import PartitionSpec as P

CHUNK = 128
KERNEL = 4
F32 = jnp.float32
BF16 = jnp.bfloat16
highest = lax.Precision.HIGHEST


def passed_along(block, axis, distance):
    devices = range(lax.axis_size(axis))
    route = [(i - distance, i) for i in devices if i - distance in devices]
    return lax.ppermute(block, axis, route)


def widen(columns, width):
    rows, heads = columns.shape
    lane = lax.broadcasted_iota(jnp.int32, (rows, 2 * width), 1)
    parts = []
    for h in range(0, heads, 2):
        left = jnp.broadcast_to(columns[:, h : h + 1], (rows, 2 * width))
        right = jnp.broadcast_to(columns[:, h + 1 : h + 2], (rows, 2 * width))
        parts.append(jnp.where(lane < width, left, right))
    return jnp.concatenate(parts, axis=1)


def conv_state_kernel(width, x_ref, before_ref, taps_ref, weight_ref, total_ref, b_ref, conv_ref, state_ref, pad_ref):
    rows = x_ref.shape[0]
    pad_ref[0:8, :] = before_ref[...]
    pad_ref[8 : 8 + rows, :] = x_ref[...]
    for r in range(0, rows, CHUNK):
        acc = taps_ref[0:1, :] * pad_ref[r + 5 : r + 5 + CHUNK, :]
        for k in range(1, KERNEL):
            acc = acc + taps_ref[k : k + 1, :] * pad_ref[r + 5 + k : r + 5 + k + CHUNK, :]
        value = acc / (1.0 + jnp.exp(-acc))
        conv_ref[r : r + CHUNK, :] = value
        fresh = (value * widen(weight_ref[0, r : r + CHUNK, :], width)).astype(BF16)
        part = lax.dot_general(
            b_ref[r : r + CHUNK, :], fresh, (((0,), (0,)), ((), ())), preferred_element_type=F32
        )
        state = part if r == 0 else state + part
    n = state.shape[0]
    state_ref[0:n, :] = state.astype(BF16)
    decay = jnp.broadcast_to(jnp.exp(total_ref[0]), (16, total_ref.shape[2]))
    state_ref[n : n + 16, :] = widen(decay, width).astype(BF16)


def local_kernel(width, x_ref, step_ref, cum_ref, cumt_ref, b_ref, c_ref, skip_ref, y_ref):
    rows, cols = x_ref.shape
    heads = cols // width
    t = lax.broadcasted_iota(jnp.int32, (CHUNK, CHUNK), 0)
    s = lax.broadcasted_iota(jnp.int32, (CHUNK, CHUNK), 1)
    lower = t >= s
    lane = lax.broadcasted_iota(jnp.int32, (CHUNK, 2 * width), 1)
    skip = widen(jnp.broadcast_to(skip_ref[0], (8, heads)), width)[0:1, :]
    state = None
    base = jnp.zeros((1, heads), F32)
    for r in range(0, rows, CHUNK):
        x = x_ref[r : r + CHUNK, :]
        b = b_ref[r : r + CHUNK, :]
        c = c_ref[r : r + CHUNK, :]
        cum = cum_ref[0, r : r + CHUNK, :]
        scaled = x * widen(step_ref[0, r : r + CHUNK, :], width)
        narrow = scaled.astype(BF16)
        scores = lax.dot_general(c, b, (((1,), (1,)), ((), ())), preferred_element_type=F32)
        scores = jnp.where(lower, scores, 0.0)
        pieces = []
        for h in range(0, heads, 2):
            pair = narrow[:, h * width : (h + 2) * width]
            both = []
            for g in (h, h + 1):
                spread = cum[:, g : g + 1] - cumt_ref[0, g : g + 1, r : r + CHUNK]
                within = scores * jnp.exp(jnp.minimum(spread, 0.0))
                both.append(jnp.dot(within.astype(BF16), pair, preferred_element_type=F32))
            pieces.append(jnp.where(lane < width, both[0], both[1]))
        y = jnp.concatenate(pieces, axis=1) + skip * x
        last = cum_ref[0, r + CHUNK - 1 : r + CHUNK, :]
        if state is not None:
            y = y + jnp.dot(c, state.astype(BF16), preferred_element_type=F32) * widen(
                jnp.exp(cum - base), width
            )
        y_ref[r : r + CHUNK, :] = y
        if r + CHUNK < rows:
            rest = (scaled * widen(jnp.exp(last - cum), width)).astype(BF16)
            fresh = lax.dot_general(b, rest, (((0,), (0,)), ((), ())), preferred_element_type=F32)
            if state is None:
                state = fresh
            else:
                kept = widen(jnp.broadcast_to(jnp.exp(last - base), (8, heads)), width)[0:1, :]
                state = kept * state + fresh
            base = last


def gate_kernel(width, y_ref, z_ref, grow_ref, c_ref, state_ref, gain_ref, out_ref, sq_ref):
    j = pl.program_id(0)

    @pl.when(j == 0)
    def _():
        sq_ref[...] = jnp.zeros_like(sq_ref)

    for r in range(0, y_ref.shape[0], CHUNK):
        at = slice(r, r + CHUNK)
        carried = jnp.dot(c_ref[at, :], state_ref[...], preferred_element_type=F32)
        ssd = y_ref[at, :] + carried * widen(grow_ref[0, at, :], width)
        z = z_ref[at, :]
        gated = ssd * (z / (1.0 + jnp.exp(-z)))
        sq_ref[at, :] += jnp.sum(gated * gated, axis=1, keepdims=True)
        out_ref[at, :] = (gated * gain_ref[...]).astype(BF16)


def per_device(
    tokens, w_in_x, w_in_z, w_in_bc, w_dt, conv_x, conv_bc, dt_bias, decay_rate, skip, norm_gain, w_out
):
    cols = w_in_x.shape[1]
    heads = dt_bias.shape[0]
    width = cols // heads
    n = w_in_bc.shape[1] // 2
    inner = cols * lax.axis_size("head")
    rows_all = lax.all_gather(tokens, "head", axis=0, tiled=True)
    rows = rows_all.shape[0]
    dot = functools.partial(jnp.dot, preferred_element_type=F32)
    x_proj = dot(rows_all, w_in_x)
    small = dot(rows_all, jnp.concatenate([w_in_bc, w_dt], axis=1))
    bc_proj, step_raw = small[:, : 2 * n], small[:, 2 * n :]
    before = passed_along(
        jnp.concatenate([x_proj[-8:], bc_proj[-8:]], axis=1), "seq", 1
    )
    x_before, bc_before = before[:, :cols], before[:, cols:]
    padded = jnp.concatenate([bc_before, bc_proj], axis=0)
    bc = sum(conv_bc[k] * padded[5 + k : 5 + k + rows] for k in range(KERNEL))
    bc = jax.nn.silu(bc).astype(BF16)
    b_mat, c_mat = bc[:, :n], bc[:, n:]
    step = jax.nn.softplus(step_raw + dt_bias)
    order = jnp.arange(rows)
    tri = (order[:, None] >= order[None, :]).astype(F32)
    cumul = jnp.dot(tri, -step * decay_rate, precision=highest)
    total = cumul[-1:]

    hb = min(heads, 256 // width)
    blocks = heads // hb
    wide = hb * width

    def by_block(a):
        return a.reshape(a.shape[0], blocks, hb).transpose(1, 0, 2)

    total3 = by_block(total)
    full = lambda r: pl.BlockSpec((r, wide), lambda j: (0, j))
    same = lambda r, c: pl.BlockSpec((r, c), lambda j: (0, 0))
    lead = lambda r, c: pl.BlockSpec((1, r, c), lambda j: (j, 0, 0))
    x_conv, packed = pl.pallas_call(
        functools.partial(conv_state_kernel, width),
        grid=(blocks,),
        in_specs=[full(rows), full(8), full(KERNEL), lead(rows, hb), lead(1, hb), same(rows, n)],
        out_specs=[full(rows), full(n + 16)],
        out_shape=[
            jax.ShapeDtypeStruct((rows, cols), F32),
            jax.ShapeDtypeStruct((n + 16, cols), BF16),
        ],
        scratch_shapes=[pltpu.VMEM((rows + 8, wide), F32)],
        cost_estimate=pl.CostEstimate(
            flops=2 * rows * n * cols, bytes_accessed=8 * rows * cols, transcendentals=rows * cols
        ),
        name="conv_state",
    )(x_proj, x_before, conv_x, by_block(step * jnp.exp(total - cumul)), total3, b_mat)

    carry = passed_along(packed, "seq", 1)
    distance = 1
    while distance < lax.axis_size("seq") - 1:
        earlier = passed_along(carry, "seq", distance).astype(F32)
        mine = carry.astype(F32)
        decay = mine[n : n + 1]
        state = decay * earlier[:n] + mine[:n]
        carry = jnp.concatenate([state, decay * earlier[n:]], axis=0).astype(BF16)
        distance *= 2
    entering = carry[:n]

    y_local = pl.pallas_call(
        functools.partial(local_kernel, width),
        grid=(blocks,),
        in_specs=[
            full(rows), lead(rows, hb), lead(rows, hb), lead(hb, rows),
            same(rows, n), same(rows, n), lead(1, hb),
        ],
        out_specs=full(rows),
        out_shape=jax.ShapeDtypeStruct((rows, cols), F32),
        cost_estimate=pl.CostEstimate(
            flops=8 * rows * n * cols, bytes_accessed=8 * rows * cols, transcendentals=rows * CHUNK * heads
        ),
        name="local_ssd",
    )(
        x_conv, by_block(step), by_block(cumul), cumul.T.reshape(blocks, hb, rows),
        b_mat, c_mat, by_block(skip[None, :]),
    )
    gate_proj = dot(rows_all, w_in_z)

    gated, squares = pl.pallas_call(
        functools.partial(gate_kernel, width),
        grid=(blocks,),
        in_specs=[
            full(rows), full(rows), lead(rows, hb), same(rows, n), full(n), full(1),
        ],
        out_specs=[full(rows), same(rows, 1)],
        out_shape=[
            jax.ShapeDtypeStruct((rows, cols), BF16),
            jax.ShapeDtypeStruct((rows, 1), F32),
        ],
        cost_estimate=pl.CostEstimate(
            flops=2 * rows * n * cols, bytes_accessed=10 * rows * cols, transcendentals=rows * cols
        ),
        name="gate",
    )(y_local, gate_proj, by_block(jnp.exp(cumul)), c_mat, entering, norm_gain[None, :])
    squares = lax.psum(squares[:, 0], "head")
    scale = lax.rsqrt(squares / inner + 1e-05)
    partial = (dot(gated, w_out) * scale[:, None]).astype(BF16)
    return lax.psum_scatter(partial, "head", scatter_dimension=0, tiled=True)


def solution(mesh):
    placed = (
        P(("seq", "head"), None), P(None, "head"), P(None, "head"), P(), P(None, "head"),
        P(None, "head"), P(), P("head"), P("head"), P("head"), P("head"), P("head", None),
    )
    return jax.shard_map(
        per_device, mesh=mesh, in_specs=placed, out_specs=P(("seq", "head"), None), check_vma=False
    )
```

time: 289 us -> 173 us (0.60); the launches traced: 283 us -> 170 us
  local copies, waits for them, and re-layouts: 67.2 us -> 14.3 us
  matrix products: 50 us -> 21.4 us
  waiting for transfers between devices: 105 us -> 84 us
  Pallas kernels: 0 us -> 20 us
  blocking collectives: 25 us -> 5.98 us
  other arithmetic: 18.9 us -> 4.41 us
  starting transfers between devices: 2.97 us -> 6.61 us
    all_gather x2 -> x1, waiting for transfers between devices: 71.2 us -> 22.6 us  [per_device(): rows_all = lax.all_gather(tokens, 'head', axis=0, tiled=True)]
    dynamic_update_slice x4 -> x0, local copies, waits for them, and re-layouts: 45.9 us -> none  [per_device(): lax.scan(advance, (empty_state, empty_decay), (x_conv.reshape(spans, SPAN...]
    dot_general x14 -> x5, matrix products: 50 us -> 21.4 us  [the longest x1 6.46 us: per_device(): gate_proj = dot(rows_all, w_in_z)]
    ppermute x2 -> x5, waiting for transfers between devices: 1.16 us -> 27.3 us  [passed_along(): return lax.ppermute(block, axis, route)]
    pallas_call x0 -> x3, Pallas kernels: none -> 20 us  [the longest x1 7.76 us: per_device(): pl.pallas_call(functools.partial(local_kernel, width), grid=(blocks,), in...]
    unnamed x1 -> x0, blocking collectives: 18.6 us -> none
    select_n x8 -> x1, other arithmetic: 9.44 us -> 0.15 us  [per_device(): step = jax.nn.softplus(step_raw + dt_bias)]
    mul x2 -> x1, other arithmetic: 7.62 us -> 0.89 us  [per_device(): step * jnp.exp(total - cumul)]
  transfers between devices with their start and end apart: 5 -> 7, of which waited for: 4 -> 5; matrix products, arithmetic and copies ran while one was open for 5% -> 11% of each run, Pallas kernels for 0% -> 5%
where the time goes in v1:
time: 173 us; the launch traced here: 170 us
  waiting for transfers between devices  84 us (49%)
  matrix products  21.4 us (12%)
  Pallas kernels  20 us (12%)
  local copies, waits for them, and re-layouts  14.3 us (8%)
  between operations  13.7 us (8%)
  starting transfers between devices  6.61 us (4%)
  blocking collectives  5.98 us (3%)
  other arithmetic  4.41 us (3%)
    reduce_scatter x1, waiting for transfers between devices, per_device(): return lax.psum_scatter(partial, 'head', scatter_dimension=0, tiled=True)  33.4 us
    ppermute x5, waiting for transfers between devices, passed_along(): return lax.ppermute(block, axis, route)  27.3 us
    all_gather x1, waiting for transfers between devices, per_device(): rows_all = lax.all_gather(tokens, 'head', axis=0, tiled=True)  22.6 us
    pallas_call x1, Pallas kernels, per_device(): pl.pallas_call(functools.partial(local_kernel, width), grid=(blocks,), in...  7.76 us
    ppermute x5, starting transfers between devices, passed_along(): return lax.ppermute(block, axis, route)  6.57 us
    pallas_call x1, Pallas kernels, per_device(): pl.pallas_call(functools.partial(gate_kernel, width), grid=(blocks,), in_...  6.51 us
    dot_general x1, matrix products, per_device(): gate_proj = dot(rows_all, w_in_z)  6.46 us
    dot_general x1, matrix products, per_device(): partial = (dot(gated, w_out) * scale[:, None]).astype(BF16)  6.18 us
  transfers between devices with their start and end apart: 7, of which 5 were waited for; matrix products, arithmetic and copies ran while one was open for 11% of the time, Pallas kernels for 5%

profile of v1, /device:TPU:28, one launch (start us, length us, event | category | flops | bytes accessed | tf_op | source)
XLA Modules:
  0.0 170.4 jit_solution(14822653909871852464)
XLA Ops:
  6.5 0.7 all-gather.2.cloned.1.call-update
  7.3 0.0 reduce-scatter.2.cloned.1.call-start
  7.3 1.1 copy.31
  8.4 1.4 fusion.28
  9.9 22.6 %all-gather.2.cloned.1.call-done = bf16[512,2048]{1,0:T(8,128)(2,1)} async-done(((bf16[128,2048]{1,0:T(8,128)(2,1)}), bf16[512,2048]{1,0:T(8,128)(2,1)}) %all-gather.2.cloned.1.call-update) | async-done | bytes 2097168 | tf_op jit(solution)/shard_map/all_gather | solution.py:125
  32.4 3.1 %fusion.4 = f32[512,272]{1,0:T(8,128)S(1)} fusion(bf16[512,2048]{1,0:T(8,128)(2,1)} %all-gather.2.cloned.1.call-done, bf16[2048,16]{1,0:T(8,128)(2,1)S(1)} %copy.31, bf16[2048,256]{1,0:T(8,128)(2,1)} %param.15), kind=kOutput, calls=%fused_computation.5 | convolution fusion | flops 572653568 | bytes 3768320 | tf_op jit(solution)/shard_map/dot_general | solution.py:129
  35.5 0.2 compare_select_fusion
  35.7 0.7 copy-done.1
  36.4 0.5 fusion.29
  36.9 0.2 slice_reduce_fusion
  37.1 0.1 copy.35
  37.2 5.2 %fusion.30.x_ref = f32[512,1024]{1,0:T(8,128)S(1)} fusion(bf16[512,2048]{1,0:T(8,128)(2,1)} %all-gather.2.cloned.1.call-done, bf16[2048,1024]{1,0:T(8,128)(2,1)} %param.13), kind=kOutput, calls=%fused_computation.49 | convolution fusion | flops 2147483648 | bytes 8388608 | tf_op jit(solution)/shard_map/dot_general | solution.py:128
  42.4 1.3 collective-permute-start
  43.7 0.9 exponential_multiply_fusion
  44.7 1.3 transpose_reshape.3
  45.9 1.0 copy.36
  47.0 1.4 copy.37
  48.4 1.0 multiply_convert_fusion.1
  49.4 0.7 fusion.27
  50.1 0.6 slice.120.before_ref
  50.7 5.7 %conv_state.1 = (f32[512,1024]{1,0:T(8,128)}, bf16[144,1024]{1,0:T(8,128)(2,1)}) custom-call(f32[512,1024]{1,0:T(8,128)} %copy-done, f32[8,1024]{1,0:T(8,128)} %slice.120.before_ref, f32[4,1024]{1,0:T(4,128)} %taps_ref.1, f32[4,512,4]{2,1,0:T(8,128)} %bitcast.32, f32[4,1,4]{2,1,0:T(1,128)} %bitcast.43, bf16[512,128]{1,0:T(8,128)(2,1)} %get-tuple-element.18.b_ref), custom_call_target="tpu_custom_call" | custom-call | flops 134217728 | bytes 4194304 | tf_op jit(solution)/shard_map/conv_state/pallas_call | solution.py:156
  56.5 1.3 collective-permute-start.1
  57.8 10.6 %collective-permute-done.1 = bf16[144,1024]{1,0:T(8,128)(2,1)S(1)} collective-permute-done((bf16[144,1024]{1,0:T(8,128)(2,1)}, bf16[144,1024]{1,0:T(8,128)(2,1)S(1)}, u32[]{:S(2)}, u32[]{:S(2)}) %collective-permute-start.1) | collective-permute-done | bytes 294944 | tf_op jit(solution)/shard_map/ppermute | solution.py:19
  68.3 1.3 collective-permute-start.2
  69.6 0.0 copy-start.5
  69.7 9.4 %collective-permute-done.2 = bf16[144,1024]{1,0:T(8,128)(2,1)S(1)} collective-permute-done((bf16[144,1024]{1,0:T(8,128)(2,1)S(1)}, bf16[144,1024]{1,0:T(8,128)(2,1)S(1)}, u32[]{:S(2)}, u32[]{:S(2)}) %collective-permute-start.2) | collective-permute-done | bytes 294944 | tf_op jit(solution)/shard_map/ppermute | solution.py:19
  79.2 0.1 fusion.17
  79.3 0.1 fusion.26
  79.4 1.3 collective-permute-start.3
  80.7 0.7 transpose_reshape_broadcast_in_dim.3
  81.3 7.3 %collective-permute-done.3 = bf16[144,1024]{1,0:T(8,128)(2,1)S(1)} collective-permute-done((bf16[144,1024]{1,0:T(8,128)(2,1)S(1)}, bf16[144,1024]{1,0:T(8,128)(2,1)S(1)}, u32[]{:S(2)}, u32[]{:S(2)}) %collective-permute-start.3) | collective-permute-done | bytes 294944 | tf_op jit(solution)/shard_map/ppermute | solution.py:19
  88.7 0.1 fusion.16
  88.8 0.1 pad_maximum_fusion.2
  88.9 1.4 collective-permute-start.4
  90.4 6.5 %fusion.31.z_ref = f32[512,1024]{1,0:T(8,128)} fusion(bf16[512,2048]{1,0:T(8,128)(2,1)} %all-gather.2.cloned.1.call-done, bf16[2048,1024]{1,0:T(8,128)(2,1)} %param.14), kind=kOutput, calls=%fused_computation.50 | convolution fusion | flops 2147483648 | bytes 8388608 | tf_op jit(solution)/shard_map/dot_general | solution.py:200
  96.8 0.1 copy.39
  96.9 1.5 copy.41
  98.4 0.6 reshape.21.cumt_ref
  99.0 1.4 copy.40
  100.4 1.4 copy.43
  101.8 7.8 %local_ssd.1.y_ref = f32[512,1024]{1,0:T(8,128)} custom-call(f32[512,1024]{1,0:T(8,128)} %get-tuple-element.9.x_ref, f32[4,512,4]{2,1,0:T(8,128)} %bitcast.35, f32[4,512,4]{2,1,0:T(8,128)} %bitcast.34, f32[4,4,512]{2,1,0:T(4,128)} %reshape.21.cumt_ref, bf16[512,128]{1,0:T(8,128)(2,1)} %get-tuple-element.18.b_ref, bf16[512,128]{1,0:T(8,128)(2,1)} %get-tuple-element.17.c_ref, ...), custom_call_target="tpu_custom_call" | custom-call | flops 536870912 | bytes 4194304 | tf_op jit(solution)/shard_map/local_ssd/pallas_call | solution.py:183
  109.6 0.8 fusion.15.state_ref
  110.4 6.5 %gate.1 = (bf16[512,1024]{1,0:T(8,128)(2,1)}, f32[512,1]{1,0:T(8,128)}) custom-call(f32[512,1024]{1,0:T(8,128)} %local_ssd.1.y_ref, f32[512,1024]{1,0:T(8,128)} %fusion.31.z_ref, f32[4,512,4]{2,1,0:T(8,128)} %bitcast.33, bf16[512,128]{1,0:T(8,128)(2,1)} %get-tuple-element.17.c_ref, bf16[128,1024]{1,0:T(8,128)(2,1)} %fusion.15.state_ref, f32[1,1024]{1,0:T(1,128)} %bitcast.44), custom_call_target="tpu_custom_call" | custom-call | flops 134217728 | bytes 5242880 | tf_op jit(solution)/shard_map/gate/pallas_call | solution.py:202
  116.9 1.1 reduce.2
  118.0 6.0 %psum.7 = f32[512]{0:T(512)S(1)} all-reduce(f32[512]{0:T(512)S(1)} %reduce.2), channel_id=1, replica_groups=mesh['seq'=8,'head'=4] {'head'}, use_global_device_ids=true, to_apply=%region_0.1 | all-reduce | flops 512 | bytes 4096 | tf_op jit(solution)/shard_map/psum | solution.py:218
  123.9 6.2 %multiply_convert_fusion = bf16[512,2048]{1,0:T(8,128)(2,1)} fusion(bf16[512,1024]{1,0:T(8,128)(2,1)} %get-tuple-element.11, bf16[1024,2048]{1,0:T(8,128)(2,1)} %param.23, f32[512]{0:T(512)S(1)} %add_rsqrt_fusion), kind=kOutput, calls=%fused_computation | convolution fusion | flops 2149580800 | bytes 7342080 | tf_op jit(solution)/shard_map/dot_general | solution.py:220
  130.1 0.0 reduce-scatter.2.cloned.1.call-update
  130.1 33.4 %reduce-scatter.2.cloned.1.call-done = bf16[128,2048]{1,0:T(8,128)(2,1)} async-done(((bf16[512,2048]{1,0:T(8,128)(2,1)}), bf16[128,2048]{1,0:T(8,128)(2,1)}) %reduce-scatter.2.cloned.1.call-update) | async-done | bytes 524304 | tf_op jit(solution)/shard_map/reduce_scatter | solution.py:221
  (33 shorter events, 0.3 us)
Async XLA Ops:
  6.5 25.9 %all-gather.2.cloned.1.call-start = ((), (), s32[]{:S(2)}) async-start(), calls=%async_computation.1 | async-start | bytes 2621440 | tf_op jit(solution)/shard_map/all_gather | solution.py:125
  7.3 156.3 %reduce-scatter.2.cloned.1.call-start = ((), (), s32[]{:S(2)}) async-start(), calls=%async_computation.2 | async-start | bytes 2621440 | tf_op jit(solution)/shard_map/reduce_scatter | solution.py:221
  9.8 25.7 %copy-start.4 = (f32[16]{0:T(128)S(1)}, f32[16]{0:T(128)}, u32[]{:S(2)}) copy-start(f32[16]{0:T(128)} %param.19) | copy-start | bytes 196
  9.9 26.5 %copy-start.6 = (f32[16]{0:T(128)S(1)}, f32[16]{0:T(128)}, u32[]{:S(2)}) copy-start(f32[16]{0:T(128)} %param.20) | copy-start | bytes 196
  35.7 0.7 copy-start.1
  37.1 6.6 %copy-start.3 = (f32[16]{0:T(128)}, f32[16]{0:T(128)S(1)}, u32[]{:S(2)}) copy-start(f32[16]{0:T(128)S(1)} %slice_reduce_fusion) | copy-start | bytes 196
  42.4 7.0 %copy-start = (f32[512,1024]{1,0:T(8,128)}, f32[512,1024]{1,0:T(8,128)S(1)}, u32[]{:S(2)}) copy-start(f32[512,1024]{1,0:T(8,128)S(1)} %fusion.30.x_ref) | copy-start | bytes 6291460
  42.4 6.0 %collective-permute-start = (f32[8,1280]{1,0:T(8,128)S(1)}, f32[8,1280]{1,0:T(8,128)S(1)}, u32[]{:S(2)}, u32[]{:S(2)}) collective-permute-start(f32[8,1280]{1,0:T(8,128)S(1)} %pad_maximum_fusion.3), channel_id=1, source_target_pairs={{0,4},{4,8},{8,12},{12,16},{16,20},{20,24},{24,28},{1,5},{5,9},{9,... | collective-permute-start | bytes 122888 | tf_op jit(solution)/shard_map/ppermute | solution.py:19
  56.5 11.9 %collective-permute-start.1 = (bf16[144,1024]{1,0:T(8,128)(2,1)}, bf16[144,1024]{1,0:T(8,128)(2,1)S(1)}, u32[]{:S(2)}, u32[]{:S(2)}) collective-permute-start(bf16[144,1024]{1,0:T(8,128)(2,1)} %get-tuple-element.10), channel_id=1, source_target_pairs={{0,4},{4,8},{8,12},{12,16},{16,20},{20,24},{24,28},{1,5},{5,9},{9,... | collective-permute-start | bytes 884744 | tf_op jit(solution)/shard_map/ppermute | solution.py:19
  68.3 10.8 %collective-permute-start.2 = (bf16[144,1024]{1,0:T(8,128)(2,1)S(1)}, bf16[144,1024]{1,0:T(8,128)(2,1)S(1)}, u32[]{:S(2)}, u32[]{:S(2)}) collective-permute-start(bf16[144,1024]{1,0:T(8,128)(2,1)S(1)} %collective-permute-done.1), channel_id=1, source_target_pairs={{0,4},{4,8},{8,12},{12,16},{16,20},{20,24},{24,28},{1,5},{5,9},{9,... | collective-permute-start | bytes 884744 | tf_op jit(solution)/shard_map/ppermute | solution.py:19
  69.6 11.0 %copy-start.5 = (f32[16]{0:T(128)S(1)}, f32[16]{0:T(128)}, u32[]{:S(2)}) copy-start(f32[16]{0:T(128)} %param.21) | copy-start | bytes 196
  79.4 9.3 %collective-permute-start.3 = (bf16[144,1024]{1,0:T(8,128)(2,1)S(1)}, bf16[144,1024]{1,0:T(8,128)(2,1)S(1)}, u32[]{:S(2)}, u32[]{:S(2)}) collective-permute-start(bf16[144,1024]{1,0:T(8,128)(2,1)S(1)} %get-tuple-element.16), channel_id=1, source_target_pairs={{0,8},{4,12},{8,16},{12,20},{16,24},{20,28},{1,9},{5,13},{9,17},{1... | collective-permute-start | bytes 884744 | tf_op jit(solution)/shard_map/ppermute | solution.py:19
  88.9 7.9 %copy-start.2 = (f32[512,16]{1,0:T(8,128)S(1)}, f32[512,16]{1,0:T(8,128)}, u32[]{:S(2)}) copy-start(f32[512,16]{1,0:T(8,128)} %copy-done.1) | copy-start | bytes 98308
  88.9 20.6 %collective-permute-start.4 = (bf16[144,1024]{1,0:T(8,128)(2,1)S(1)}, bf16[144,1024]{1,0:T(8,128)(2,1)S(1)}, u32[]{:S(2)}, u32[]{:S(2)}) collective-permute-start(bf16[144,1024]{1,0:T(8,128)(2,1)S(1)} %get-tuple-element.13), channel_id=1, source_target_pairs={{0,16},{4,20},{8,24},{12,28},{1,17},{5,21},{9,25},{13,29},{2,18},{... | collective-permute-start | bytes 884744 | tf_op jit(solution)/shard_map/ppermute | solution.py:19
Sparse Core Ops, SparseCore 0:
  8.9 23.4 all-gather.1
  130.3 33.2 reduce-scatter.1

commit v2 on v1

--- a/solution.py
+++ b/solution.py
@@ -114,6 +114,168 @@
         out_ref[at, :] = (gated * gain_ref[...]).astype(BF16)
 
 
+MESH = pl.DeviceIdType.MESH
+PIECES = 4
+
+
+def greet(peers):
+    barrier = pltpu.get_barrier_semaphore()
+    for peer in peers:
+        pl.semaphore_signal(barrier, inc=1, device_id={"head": peer}, device_id_type=MESH)
+    pl.semaphore_wait(barrier, len(peers))
+
+
+def gather_kernel(n, x_ref, out_ref, send_own, recv_own, send_far, recv_far, send_on, recv_on):
+    me = lax.axis_index("head")
+    half = n // 2
+    chip, core = me // 2, me % 2
+    partner = chip * 2 + 1 - core
+    rows = x_ref.shape[0]
+    part = rows // PIECES
+    far = [lax.rem(chip + d, half) * 2 + core for d in range(1, half)]
+    greet([partner] + far)
+
+    def remote(src, dst, ssem, rsem, to):
+        return pltpu.make_async_remote_copy(
+            src_ref=src, dst_ref=dst, send_sem=ssem, recv_sem=rsem,
+            device_id={"head": to}, device_id_type=MESH,
+        )
+
+    def place(owner, q):
+        return out_ref.at[pl.ds(pl.multiple_of(owner * rows + q * part, part), part), :]
+
+    sent = []
+    for q in range(PIECES):
+        for d in range(1, half):
+            sent.append(
+                remote(x_ref.at[pl.ds(q * part, part), :], place(me, q),
+                       send_far.at[d, q], recv_far.at[d, q], far[d - 1])
+            )
+            sent[-1].start()
+    for q in range(PIECES):
+        sent.append(
+            remote(x_ref.at[pl.ds(q * part, part), :], place(me, q),
+                   send_own.at[q], recv_own.at[q], partner)
+        )
+        sent[-1].start()
+    out_ref[pl.ds(pl.multiple_of(me * rows, rows), rows), :] = x_ref[...]
+    passed = []
+    for q in range(PIECES):
+        for d in range(1, half):
+            owner = lax.rem(chip - d + half, half) * 2 + core
+            remote(place(owner, q), place(owner, q), send_far.at[d, q], recv_far.at[d, q], partner).wait_recv()
+            passed.append(
+                remote(place(owner, q), place(owner, q), send_on.at[d, q], recv_on.at[d, q], partner)
+            )
+            passed[-1].start()
+    for copy in sent:
+        copy.wait_send()
+    for q in range(PIECES):
+        remote(place(partner, q), place(partner, q), send_own.at[q], recv_own.at[q], partner).wait_recv()
+    for copy in passed:
+        copy.wait_send()
+    for q in range(PIECES):
+        for d in range(1, half):
+            owner = lax.rem(chip - d + half, half) * 2 + 1 - core
+            remote(place(owner, q), place(owner, q), send_on.at[d, q], recv_on.at[d, q], partner).wait_recv()
+
+
+def gather_tokens(tokens, n):
+    rows, depth = tokens.shape
+    half = n // 2
+    dma = pltpu.SemaphoreType.DMA
+    return pl.pallas_call(
+        functools.partial(gather_kernel, n),
+        out_shape=jax.ShapeDtypeStruct((rows * n, depth), tokens.dtype),
+        in_specs=[pl.BlockSpec(memory_space=pltpu.VMEM)],
+        out_specs=pl.BlockSpec(memory_space=pltpu.VMEM),
+        scratch_shapes=[dma((PIECES,)), dma((PIECES,))] + [dma((half, PIECES))] * 4,
+        compiler_params=pltpu.CompilerParams(collective_id=0, has_side_effects=True),
+        name="gather_tokens",
+    )(tokens)
+
+
+def scatter_kernel(n, p_ref, sq_ref, out_ref, total_ref, got, summed, landed, squares, s1, r1, s2, r2, s3, r3):
+    me = lax.axis_index("head")
+    half = n // 2
+    chip, core = me // 2, me % 2
+    partner = chip * 2 + 1 - core
+    rows = out_ref.shape[0]
+    part = rows // PIECES
+    peers = [lax.rem(me + d, n) for d in range(1, n)]
+    greet(peers)
+
+    def remote(src, dst, ssem, rsem, to):
+        return pltpu.make_async_remote_copy(
+            src_ref=src, dst_ref=dst, send_sem=ssem, recv_sem=rsem,
+            device_id={"head": to}, device_id_type=MESH,
+        )
+
+    def block(owner, q):
+        return p_ref.at[pl.ds(pl.multiple_of(owner * rows + q * part, part), part), :]
+
+    def piece(ref, d, q):
+        return ref.at[d, pl.ds(q * part, part), :]
+
+    sent = []
+    for d in list(range(1, half)) + [0]:
+        for q in range(PIECES):
+            owner = lax.rem(chip + d, half) * 2 + 1 - core
+            sent.append(remote(block(owner, q), piece(got, d, q), s1.at[d, q], r1.at[d, q], partner))
+            sent[-1].start()
+    for d in range(1, n):
+        sent.append(remote(sq_ref.at[peers[d - 1]], squares.at[d], s3.at[d], r3.at[d], peers[d - 1]))
+        sent[-1].start()
+    for d in range(1, half):
+        for q in range(PIECES):
+            owner = lax.rem(chip + d, half) * 2 + core
+            remote(piece(got, d, q), piece(got, d, q), s1.at[d, q], r1.at[d, q], partner).wait_recv()
+            both = block(owner, q)[...].astype(F32) + piece(got, d, q)[...].astype(F32)
+            summed[d, q * part : (q + 1) * part, :] = both.astype(BF16)
+            sent.append(remote(piece(summed, d, q), piece(landed, d, q), s2.at[d, q], r2.at[d, q], owner))
+            sent[-1].start()
+    total = sq_ref[me]
+    for d in range(1, n):
+        remote(squares.at[d], squares.at[d], s3.at[d], r3.at[d], partner).wait_recv()
+        total = total + squares[d]
+    total_ref[...] = total
+    for q in range(PIECES):
+        remote(piece(got, 0, q), piece(got, 0, q), s1.at[0, q], r1.at[0, q], partner).wait_recv()
+        out_ref[q * part : (q + 1) * part, :] = (
+            block(me, q)[...].astype(F32) + piece(got, 0, q)[...].astype(F32)
+        )
+    for q in range(PIECES):
+        for d in range(1, half):
+            remote(piece(landed, d, q), piece(landed, d, q), s2.at[d, q], r2.at[d, q], partner).wait_recv()
+            out_ref[q * part : (q + 1) * part, :] += piece(landed, d, q)[...].astype(F32)
+    for copy in sent:
+        copy.wait_send()
+
+
+def scatter_sum(partial, squares, n):
+    rows, depth = partial.shape
+    rows = rows // n
+    half = n // 2
+    dma = pltpu.SemaphoreType.DMA
+    vmem = pl.BlockSpec(memory_space=pltpu.VMEM)
+    squares = jnp.broadcast_to(squares.reshape(n, 1, rows), (n, 8, rows))
+    return pl.pallas_call(
+        functools.partial(scatter_kernel, n),
+        out_shape=[
+            jax.ShapeDtypeStruct((rows, depth), F32),
+            jax.ShapeDtypeStruct((8, rows), F32),
+        ],
+        in_specs=[vmem, vmem],
+        out_specs=[vmem, vmem],
+        scratch_shapes=[pltpu.VMEM((half, rows, depth), BF16)] * 3
+        + [pltpu.VMEM((n, 8, rows), F32)]
+        + [dma((half, PIECES))] * 4
+        + [dma((n,))] * 2,
+        compiler_params=pltpu.CompilerParams(collective_id=1, has_side_effects=True),
+        name="scatter_sum",
+    )(partial, squares)
+
+
 def per_device(
     tokens, w_in_x, w_in_z, w_in_bc, w_dt, conv_x, conv_bc, dt_bias, decay_rate, skip, norm_gain, w_out
 ):
@@ -122,7 +284,7 @@
     width = cols // heads
     n = w_in_bc.shape[1] // 2
     inner = cols * lax.axis_size("head")
-    rows_all = lax.all_gather(tokens, "head", axis=0, tiled=True)
+    rows_all = gather_tokens(tokens, lax.axis_size("head"))
     rows = rows_all.shape[0]
     dot = functools.partial(jnp.dot, preferred_element_type=F32)
     x_proj = dot(rows_all, w_in_x)
@@ -169,17 +331,6 @@
         name="conv_state",
     )(x_proj, x_before, conv_x, by_block(step * jnp.exp(total - cumul)), total3, b_mat)
 
-    carry = passed_along(packed, "seq", 1)
-    distance = 1
-    while distance < lax.axis_size("seq") - 1:
-        earlier = passed_along(carry, "seq", distance).astype(F32)
-        mine = carry.astype(F32)
-        decay = mine[n : n + 1]
-        state = decay * earlier[:n] + mine[:n]
-        carry = jnp.concatenate([state, decay * earlier[n:]], axis=0).astype(BF16)
-        distance *= 2
-    entering = carry[:n]
-
     y_local = pl.pallas_call(
         functools.partial(local_kernel, width),
         grid=(blocks,),
@@ -198,6 +349,20 @@
         b_mat, c_mat, by_block(skip[None, :]),
     )
     gate_proj = dot(rows_all, w_in_z)
+    fillers = [y_local, gate_proj]
+    carry = passed_along(packed, "seq", 1)
+    distance = 1
+    while distance < lax.axis_size("seq") - 1:
+        if fillers:
+            carry, done = lax.optimization_barrier((carry, fillers.pop(0)))
+            y_local, gate_proj = (done, gate_proj) if distance == 1 else (y_local, done)
+        earlier = passed_along(carry, "seq", distance).astype(F32)
+        mine = carry.astype(F32)
+        decay = mine[n : n + 1]
+        state = decay * earlier[:n] + mine[:n]
+        carry = jnp.concatenate([state, decay * earlier[n:]], axis=0).astype(BF16)
+        distance *= 2
+    entering = carry[:n]
 
     gated, squares = pl.pallas_call(
         functools.partial(gate_kernel, width),
@@ -215,10 +380,9 @@
         ),
         name="gate",
     )(y_local, gate_proj, by_block(jnp.exp(cumul)), c_mat, entering, norm_gain[None, :])
-    squares = lax.psum(squares[:, 0], "head")
-    scale = lax.rsqrt(squares / inner + 1e-05)
-    partial = (dot(gated, w_out) * scale[:, None]).astype(BF16)
-    return lax.psum_scatter(partial, "head", scatter_dimension=0, tiled=True)
+    mixed, squares = scatter_sum(dot(gated, w_out).astype(BF16), squares[:, 0], lax.axis_size("head"))
+    scale = lax.rsqrt(squares[0] / inner + 1e-05)
+    return (mixed * scale[:, None]).astype(BF16)
 
 
 def solution(mesh):

time: 173 us -> 133 us (0.77)
  waiting for transfers between devices: 84 us -> 28.3 us
  Pallas kernels: 20 us -> 56.3 us
  between operations: 13.7 us -> 0.35 us
  blocking collectives: 5.98 us -> 0 us
  other arithmetic: 4.41 us -> 6.93 us
  matrix products: 21.4 us -> 19.1 us
    pallas_call x0 -> x2, Pallas kernels: none -> 36.3 us  [the longest x1 18.4 us: scatter_sum(): pl.pallas_call(functools.partial(scatter_kernel, n), out_shape=[jax.Shape...]
    reduce_scatter x1 -> x0, waiting for transfers between devices: 33.4 us -> none  [per_device(): return lax.psum_scatter(partial, 'head', scatter_dimension=0, tiled=True)]
    all_gather x1 -> x0, waiting for transfers between devices: 22.6 us -> none  [per_device(): rows_all = lax.all_gather(tokens, 'head', axis=0, tiled=True)]
    psum x1 -> x0, blocking collectives: 5.98 us -> none  [per_device(): squares = lax.psum(squares[:, 0], 'head')]
    convert_element_type x0 -> x1, other arithmetic: none -> 2.14 us  [per_device(): return (mixed * scale[:, None]).astype(BF16)]
    dot_general x1, matrix products: 3.11 us -> 1.27 us  [per_device(): small = dot(rows_all, jnp.concatenate([w_in_bc, w_dt], axis=1))]
  transfers between devices with their start and end apart: 7 -> 5, of which waited for: 5 -> 3; matrix products, arithmetic and copies ran while one was open for 11% -> 15% of each run, Pallas kernels for 5% -> 6%
where the time goes in v2:
time: 133 us; the launch traced here: 131 us
  Pallas kernels  56.3 us (42%)
  waiting for transfers between devices  28.3 us (21%)
  matrix products  19.1 us (14%)
  local copies, waits for them, and re-layouts  13.4 us (10%)
  other arithmetic  6.93 us (5%)
  starting transfers between devices  6.63 us (5%)
    ppermute x5, waiting for transfers between devices, passed_along(): return lax.ppermute(block, axis, route)  28.3 us
    pallas_call x1, Pallas kernels, scatter_sum(): pl.pallas_call(functools.partial(scatter_kernel, n), out_shape=[jax.Shape...  18.4 us
    pallas_call x1, Pallas kernels, gather_tokens(): pl.pallas_call(functools.partial(gather_kernel, n), out_shape=jax.ShapeDt...  17.8 us
    pallas_call x1, Pallas kernels, per_device(): pl.pallas_call(functools.partial(local_kernel, width), grid=(blocks,), in...  7.77 us
    ppermute x5, starting transfers between devices, passed_along(): return lax.ppermute(block, axis, route)  6.63 us
    pallas_call x1, Pallas kernels, per_device(): pl.pallas_call(functools.partial(gate_kernel, width), grid=(blocks,), in_...  6.44 us
    dot_general x1, matrix products, per_device(): dot(gated, w_out).astype(BF16)  6.23 us
    dot_general x1, matrix products, per_device(): gate_proj = dot(rows_all, w_in_z)  5.85 us
  transfers between devices with their start and end apart: 5, of which 3 were waited for; matrix products, arithmetic and copies ran while one was open for 15% of the time, Pallas kernels for 6%

profile of v2, /device:TPU:28, one launch (start us, length us, event | category | flops | bytes accessed | tf_op | source)
XLA Modules:
  0.0 131.0 jit_solution(10000768794175403445)
XLA Ops:
  0.0 17.8 %gather_tokens.1 = bf16[512,2048]{1,0:T(8,128)(2,1)} custom-call(bf16[128,2048]{1,0:T(8,128)(2,1)} %x_ref.1), custom_call_target="tpu_custom_call" | custom-call | tf_op jit(solution)/shard_map/gather_tokens/pallas_call | solution.py:187
  17.9 0.3 copy.31
  18.2 0.0 copy-start.9
  18.2 5.3 %fusion.29.x_ref = f32[512,1024]{1,0:T(8,128)S(1)} fusion(bf16[512,2048]{1,0:T(8,128)(2,1)} %gather_tokens.1, bf16[2048,1024]{1,0:T(8,128)(2,1)} %param.13), kind=kOutput, calls=%fused_computation.49 | convolution fusion | flops 2147483648 | bytes 8388608 | tf_op jit(solution)/shard_map/dot_general | solution.py:290
  23.5 0.0 copy-start.7
  23.5 0.0 copy-start.10
  23.5 1.3 fusion.4
  24.8 0.0 copy-done
  24.8 1.3 collective-permute-start
  26.2 0.2 compare_select_fusion
  26.3 0.5 fusion.28
  26.8 0.1 copy.35
  27.0 0.2 slice_reduce_fusion
  27.2 1.6 %exponential_multiply_fusion = f32[512,16]{1,0:T(8,128)} fusion(f32[512,16]{1,0:T(8,128)S(1)} %copy.35, f32[16]{0:T(128)S(1)} %slice_reduce_fusion, f32[16]{0:T(128)} %param.19, f32[512,272]{1,0:T(8,128)S(1)} %fusion.4), kind=kLoop, calls=%fused_computation.33 | loop fusion | flops 73728 | bytes 98432 | tf_op jit(solution)/shard_map/mul | solution.py:332
  28.7 1.4 %fusion.27 = (f32[1,256]{1,0:T(1,128)}, f32[1,256]{1,0:T(1,128)}, f32[1,256]{1,0:T(1,128)}, f32[1,256]{1,0:T(1,128)}) fusion(f32[4,256]{1,0:T(4,128)} %param.18), kind=kLoop, calls=%fused_computation.47 | loop fusion | bytes 8192 | tf_op jit(solution)/shard_map/slice | solution.py:298
  30.2 1.3 %transpose_reshape.3 = f32[4,1,4]{2,0,1:T(4,128)} reshape(f32[16]{0:T(128)} %copy-done.6) | data formatting | bytes 128 | tf_op jit(solution)/shard_map/transpose;reshape | solution.py:312
  31.5 1.0 copy.36
  32.6 1.4 %copy.37 = f32[512,4,4]{2,0,1:T(8,128)} copy(f32[512,4,4]{0,2,1:T(4,128)S(1)} %reshape.30) | data formatting | bytes 65536 | tf_op jit(solution)/shard_map/reshape | solution.py:312
  34.0 1.0 multiply_convert_fusion.1
  35.0 0.7 fusion.26
  35.7 0.6 slice.124.before_ref
  36.3 5.8 %conv_state.1 = (f32[512,1024]{1,0:T(8,128)}, bf16[144,1024]{1,0:T(8,128)(2,1)}) custom-call(f32[512,1024]{1,0:T(8,128)} %copy-done, f32[8,1024]{1,0:T(8,128)} %slice.124.before_ref, f32[4,1024]{1,0:T(4,128)} %taps_ref.1, f32[4,512,4]{2,1,0:T(8,128)} %bitcast.35, f32[4,1,4]{2,1,0:T(1,128)} %bitcast.47, bf16[512,128]{1,0:T(8,128)(2,1)} %get-tuple-element.28.b_ref), custom_call_target="tpu_custom_call" | custom-call | flops 134217728 | bytes 4194304 | tf_op jit(solution)/shard_map/conv_state/pallas_call | solution.py:318
  42.1 1.3 collective-permute-start.1
  43.4 0.1 copy.39
  43.6 1.4 %copy.40 = f32[512,4,4]{2,0,1:T(8,128)} copy(f32[512,4,4]{0,2,1:T(4,128)S(1)} %reshape.31) | data formatting | bytes 65536 | tf_op jit(solution)/shard_map/reshape | solution.py:312
  44.9 1.4 %copy.41 = f32[512,4,4]{2,0,1:T(8,128)} copy(f32[512,4,4]{0,2,1:T(4,128)S(1)} %reshape.32) | data formatting | bytes 65536 | tf_op jit(solution)/shard_map/reshape | solution.py:312
  46.3 0.6 reshape.33.cumt_ref
  46.9 0.7 transpose_reshape_broadcast_in_dim.3
  47.6 7.8 %local_ssd.1.y_ref = f32[512,1024]{1,0:T(8,128)} custom-call(f32[512,1024]{1,0:T(8,128)} %get-tuple-element.16.x_ref, f32[4,512,4]{2,1,0:T(8,128)} %bitcast.37, f32[4,512,4]{2,1,0:T(8,128)} %bitcast.38, f32[4,4,512]{2,1,0:T(4,128)} %reshape.33.cumt_ref, bf16[512,128]{1,0:T(8,128)(2,1)} %get-tuple-element.28.b_ref, bf16[512,128]{1,0:T(8,128)(2,1)} %get-tuple-element.27.c_ref, ...), custom_call_target="tpu_custom_call" | custom-call | flops 536870912 | bytes 4194304 | tf_op jit(solution)/shard_map/local_ssd/pallas_call | solution.py:334
  55.3 1.3 collective-permute-start.2
  56.6 5.8 %fusion.30.z_ref = f32[512,1024]{1,0:T(8,128)} fusion(bf16[512,2048]{1,0:T(8,128)(2,1)S(1)} %copy-done.1, bf16[2048,1024]{1,0:T(8,128)(2,1)} %param.14), kind=kOutput, calls=%fused_computation.50 | convolution fusion | flops 2147483648 | bytes 8388608 | tf_op jit(solution)/shard_map/dot_general | solution.py:351
  62.5 5.2 %collective-permute-done.2 = bf16[144,1024]{1,0:T(8,128)(2,1)S(1)} collective-permute-done((bf16[144,1024]{1,0:T(8,128)(2,1)S(1)}, bf16[144,1024]{1,0:T(8,128)(2,1)S(1)}, u32[]{:S(2)}, u32[]{:S(2)}) %collective-permute-start.2) | collective-permute-done | bytes 294944 | tf_op jit(solution)/shard_map/ppermute | solution.py:19
  67.8 0.1 fusion.17
  67.9 1.3 collective-permute-start.3
  69.3 9.5 %collective-permute-done.3 = bf16[144,1024]{1,0:T(8,128)(2,1)S(1)} collective-permute-done((bf16[144,1024]{1,0:T(8,128)(2,1)S(1)}, bf16[144,1024]{1,0:T(8,128)(2,1)S(1)}, u32[]{:S(2)}, u32[]{:S(2)}) %collective-permute-start.3) | collective-permute-done | bytes 294944 | tf_op jit(solution)/shard_map/ppermute | solution.py:19
  78.9 0.1 fusion.16
  79.0 0.1 pad_maximum_fusion.2
  79.1 1.5 %collective-permute-start.4 = (bf16[144,1024]{1,0:T(8,128)(2,1)S(1)}, bf16[144,1024]{1,0:T(8,128)(2,1)S(1)}, u32[]{:S(2)}, u32[]{:S(2)}) collective-permute-start(bf16[144,1024]{1,0:T(8,128)(2,1)S(1)} %get-tuple-element.25), channel_id=1, source_target_pairs={{0,16},{4,20},{8,24},{12,28},{1,17},{5,21},{9,25},{13,29},{2,18},{... | collective-permute-start | bytes 884744 | tf_op jit(solution)/shard_map/ppermute | solution.py:19
  80.6 1.4 %copy.43 = f32[512,4,4]{2,0,1:T(8,128)} copy(f32[512,4,4]{0,2,1:T(4,128)S(1)} %reshape.34) | data formatting | bytes 65536 | tf_op jit(solution)/shard_map/reshape | solution.py:312
  82.0 13.5 %collective-permute-done.4 = bf16[144,1024]{1,0:T(8,128)(2,1)S(1)} collective-permute-done((bf16[144,1024]{1,0:T(8,128)(2,1)S(1)}, bf16[144,1024]{1,0:T(8,128)(2,1)S(1)}, u32[]{:S(2)}, u32[]{:S(2)}) %collective-permute-start.4) | collective-permute-done | bytes 294944 | tf_op jit(solution)/shard_map/ppermute | solution.py:19
  95.5 0.8 fusion.15.state_ref
  96.2 6.4 %gate.1 = (bf16[512,1024]{1,0:T(8,128)(2,1)}, f32[512,1]{1,0:T(8,128)}) custom-call(f32[512,1024]{1,0:T(8,128)} %local_ssd.1.y_ref, f32[512,1024]{1,0:T(8,128)} %fusion.30.z_ref, f32[4,512,4]{2,1,0:T(8,128)} %bitcast.36, bf16[512,128]{1,0:T(8,128)(2,1)} %get-tuple-element.27.c_ref, bf16[128,1024]{1,0:T(8,128)(2,1)} %fusion.15.state_ref, f32[1,1024]{1,0:T(1,128)} %bitcast.48), custom_call_target="tpu_custom_call" | custom-call | flops 134217728 | bytes 5242880 | tf_op jit(solution)/shard_map/gate/pallas_call | solution.py:367
  102.7 6.2 %convolution_convert_fusion.p_ref = bf16[512,2048]{1,0:T(8,128)(2,1)} fusion(bf16[512,1024]{1,0:T(8,128)(2,1)} %get-tuple-element.21, bf16[1024,2048]{1,0:T(8,128)(2,1)} %param.23), kind=kOutput, calls=%fused_computation | convolution fusion | flops 2148532224 | bytes 7340032 | tf_op jit(solution)/shard_map/dot_general | solution.py:383
  108.9 0.1 reduce.2
  109.1 0.6 broadcast_in_dim.8.sq_ref
  109.7 18.4 %scatter_sum.1 = (f32[128,2048]{1,0:T(8,128)}, f32[8,128]{1,0:T(8,128)}) custom-call(bf16[512,2048]{1,0:T(8,128)(2,1)} %convolution_convert_fusion.p_ref, f32[4,8,128]{2,1,0:T(8,128)} %broadcast_in_dim.8.sq_ref), custom_call_target="tpu_custom_call" | custom-call | tf_op jit(solution)/shard_map/scatter_sum/pallas_call | solution.py:262
  128.1 0.7 rsqrt_bitcast_fusion
  128.8 2.1 %multiply_convert_fusion = bf16[128,2048]{1,0:T(8,128)(2,1)} fusion(f32[128,2048]{1,0:T(8,128)} %get-tuple-element.23, f32[128]{0:T(128)S(1)} %rsqrt_bitcast_fusion), kind=kLoop, calls=%fused_computation.6 | loop fusion | flops 524288 | bytes 1573376 | tf_op jit(solution)/shard_map/convert_element_type | solution.py:385
  (39 shorter events, 0.4 us)
Async XLA Ops:
  0.0 17.9 %copy-start.5 = (bf16[2048,16]{0,1:T(8,128)(2,1)S(1)}, bf16[2048,16]{0,1:T(8,128)(2,1)}, u32[]{:S(2)}) copy-start(bf16[2048,16]{0,1:T(8,128)(2,1)} %param.16) | copy-start | bytes 196612
  18.1 5.3 %copy-start.1 = (bf16[512,2048]{1,0:T(8,128)(2,1)S(1)}, bf16[512,2048]{1,0:T(8,128)(2,1)}, u32[]{:S(2)}) copy-start(bf16[512,2048]{1,0:T(8,128)(2,1)} %gather_tokens.1) | copy-start | bytes 6291460
  18.2 5.3 %copy-start.9 = (bf16[2048,256]{1,0:T(8,128)(2,1)S(1)}, bf16[2048,256]{1,0:T(8,128)(2,1)}, u32[]{:S(2)}) copy-start(bf16[2048,256]{1,0:T(8,128)(2,1)} %param.15) | copy-start | bytes 3145732
  23.5 1.3 %copy-start = (f32[512,1024]{1,0:T(8,128)}, f32[512,1024]{1,0:T(8,128)S(1)}, u32[]{:S(2)}) copy-start(f32[512,1024]{1,0:T(8,128)S(1)} %fusion.29.x_ref) | copy-start | bytes 6291460
  23.5 2.6 %copy-start.7 = (f32[16]{0:T(128)S(1)}, f32[16]{0:T(128)}, u32[]{:S(2)}) copy-start(f32[16]{0:T(128)} %param.19) | copy-start | bytes 196
  23.5 2.8 %copy-start.10 = (f32[16]{0:T(128)S(1)}, f32[16]{0:T(128)}, u32[]{:S(2)}) copy-start(f32[16]{0:T(128)} %param.20) | copy-start | bytes 196
  24.8 9.1 %collective-permute-start = (f32[8,1280]{1,0:T(8,128)S(1)}, f32[8,1280]{1,0:T(8,128)S(1)}, u32[]{:S(2)}, u32[]{:S(2)}) collective-permute-start(f32[8,1280]{1,0:T(8,128)S(1)} %pad_maximum_fusion.3), channel_id=1, source_target_pairs={{0,4},{4,8},{8,12},{12,16},{16,20},{20,24},{24,28},{1,5},{5,9},{9,... | collective-permute-start | bytes 122888 | tf_op jit(solution)/shard_map/ppermute | solution.py:19
  26.3 3.8 %copy-start.2 = (f32[512,16]{1,0:T(8,128)}, f32[512,16]{1,0:T(8,128)S(1)}, u32[]{:S(2)}) copy-start(f32[512,16]{1,0:T(8,128)S(1)} %compare_select_fusion) | copy-start | bytes 98308
  27.2 1.6 %copy-start.6 = (f32[16]{0:T(128)}, f32[16]{0:T(128)S(1)}, u32[]{:S(2)}) copy-start(f32[16]{0:T(128)S(1)} %slice_reduce_fusion) | copy-start | bytes 196
  35.0 8.4 %copy-start.3 = (f32[512,16]{1,0:T(8,128)S(1)}, f32[512,16]{1,0:T(8,128)}, u32[]{:S(2)}) copy-start(f32[512,16]{1,0:T(8,128)} %copy-done.2) | copy-start | bytes 98308
  42.1 4.8 %copy-start.8 = (f32[16]{0:T(128)S(1)}, f32[16]{0:T(128)}, u32[]{:S(2)}) copy-start(f32[16]{0:T(128)} %param.21) | copy-start | bytes 196
  42.1 13.2 %collective-permute-start.1 = (bf16[144,1024]{1,0:T(8,128)(2,1)}, bf16[144,1024]{1,0:T(8,128)(2,1)S(1)}, u32[]{:S(2)}, u32[]{:S(2)}) collective-permute-start(bf16[144,1024]{1,0:T(8,128)(2,1)} %get-tuple-element.15), channel_id=1, source_target_pairs={{0,4},{4,8},{8,12},{12,16},{16,20},{20,24},{24,28},{1,5},{5,9},{9,... | collective-permute-start | bytes 884744 | tf_op jit(solution)/shard_map/ppermute | solution.py:19
  55.3 12.4 %collective-permute-start.2 = (bf16[144,1024]{1,0:T(8,128)(2,1)S(1)}, bf16[144,1024]{1,0:T(8,128)(2,1)S(1)}, u32[]{:S(2)}, u32[]{:S(2)}) collective-permute-start(bf16[144,1024]{1,0:T(8,128)(2,1)S(1)} %collective-permute-done.1), channel_id=1, source_target_pairs={{0,4},{4,8},{8,12},{12,16},{16,20},{20,24},{24,28},{1,5},{5,9},{9,... | collective-permute-start | bytes 884744 | tf_op jit(solution)/shard_map/ppermute | solution.py:19
  67.9 10.9 %collective-permute-start.3 = (bf16[144,1024]{1,0:T(8,128)(2,1)S(1)}, bf16[144,1024]{1,0:T(8,128)(2,1)S(1)}, u32[]{:S(2)}, u32[]{:S(2)}) collective-permute-start(bf16[144,1024]{1,0:T(8,128)(2,1)S(1)} %pad_maximum_fusion.1), channel_id=1, source_target_pairs={{0,8},{4,12},{8,16},{12,20},{16,24},{20,28},{1,9},{5,13},{9,17},{1... | collective-permute-start | bytes 884744 | tf_op jit(solution)/shard_map/ppermute | solution.py:19
  79.1 16.4 %collective-permute-start.4 = (bf16[144,1024]{1,0:T(8,128)(2,1)S(1)}, bf16[144,1024]{1,0:T(8,128)(2,1)S(1)}, u32[]{:S(2)}, u32[]{:S(2)}) collective-permute-start(bf16[144,1024]{1,0:T(8,128)(2,1)S(1)} %get-tuple-element.25), channel_id=1, source_target_pairs={{0,16},{4,20},{8,24},{12,28},{1,17},{5,21},{9,25},{13,29},{2,18},{... | collective-permute-start | bytes 884744 | tf_op jit(solution)/shard_map/ppermute | solution.py:19
  102.7 6.2 %copy-start.4 = (f32[512,1]{1,0:T(8,128)S(1)}, f32[512,1]{1,0:T(8,128)}, u32[]{:S(2)}) copy-start(f32[512,1]{1,0:T(8,128)} %get-tuple-element.22) | copy-start | bytes 6148

commit v3 on v2

--- a/solution.py
+++ b/solution.py
@@ -97,17 +97,11 @@
             base = last
 
 
-def gate_kernel(width, y_ref, z_ref, grow_ref, c_ref, state_ref, gain_ref, out_ref, sq_ref):
-    j = pl.program_id(0)
-
-    @pl.when(j == 0)
-    def _():
-        sq_ref[...] = jnp.zeros_like(sq_ref)
-
+def gate_block(width, y_ref, z_ref, cum_ref, c_ref, state_ref, gain_ref, out_ref, sq_ref):
     for r in range(0, y_ref.shape[0], CHUNK):
         at = slice(r, r + CHUNK)
         carried = jnp.dot(c_ref[at, :], state_ref[...], preferred_element_type=F32)
-        ssd = y_ref[at, :] + carried * widen(grow_ref[0, at, :], width)
+        ssd = y_ref[at, :] + carried * widen(jnp.exp(cum_ref[0, at, :]), width)
         z = z_ref[at, :]
         gated = ssd * (z / (1.0 + jnp.exp(-z)))
         sq_ref[at, :] += jnp.sum(gated * gated, axis=1, keepdims=True)
@@ -274,6 +268,68 @@
         compiler_params=pltpu.CompilerParams(collective_id=1, has_side_effects=True),
         name="scatter_sum",
     )(partial, squares)
+
+
+def chain_kernel(
+    n_seq, width, packed_ref, rows_ref, wz_ref, x_ref, step_ref, cum_ref, cumt_ref, b_ref, c_ref,
+    skip_ref, gain_ref, out_ref, sq_ref, y_ref, z_ref, held, came, send_sem, recv_sem,
+):
+    me = lax.axis_index("seq")
+    n = b_ref.shape[1]
+    blocks, _, hb = step_ref.shape
+    wide = hb * width
+    steps = [1]
+    while 2 * steps[-1] < n_seq:
+        steps.append(2 * steps[-1])
+    barrier = pltpu.get_barrier_semaphore()
+    for d in steps:
+        for peer in (lax.rem(me + d, n_seq), lax.rem(me - d + n_seq, n_seq)):
+            pl.semaphore_signal(barrier, inc=1, device_id={"seq": peer}, device_id_type=MESH)
+    pl.semaphore_wait(barrier, 2 * len(steps))
+
+    def z_unit(j):
+        z_ref[:, j * wide : (j + 1) * wide] = jnp.dot(
+            rows_ref[...], wz_ref[:, j * wide : (j + 1) * wide], preferred_element_type=F32
+        )
+
+    def local_unit(j):
+        at = pl.ds(j * wide, wide)
+        one = pl.ds(j, 1)
+        local_kernel(
+            width, x_ref.at[:, at], step_ref.at[one], cum_ref.at[one], cumt_ref.at[one],
+            b_ref, c_ref, skip_ref.at[one], y_ref.at[:, at],
+        )
+
+    units = [functools.partial(f, j) for j in range(blocks) for f in (local_unit, z_unit)]
+    distances = [1] + steps
+    for k, d in enumerate(distances):
+        copy = pltpu.make_async_remote_copy(
+            src_ref=packed_ref if k == 0 else held.at[k],
+            dst_ref=came.at[k], send_sem=send_sem.at[k], recv_sem=recv_sem.at[k],
+            device_id={"seq": lax.rem(me + d, n_seq)}, device_id_type=MESH,
+        )
+        copy.start()
+        first = k * len(units) // len(distances)
+        for unit in units[first : (k + 1) * len(units) // len(distances)]:
+            unit()
+        copy.wait()
+        valid = (me >= d).astype(F32)
+        for j in range(blocks):
+            at = slice(j * wide, (j + 1) * wide)
+            earlier = came[k, :, at].astype(F32) * valid
+            if k > 0:
+                mine = held[k, :, at].astype(F32)
+                decay = mine[n : n + 1]
+                earlier = jnp.concatenate([decay * earlier[:n] + mine[:n], decay * earlier[n:]], axis=0)
+            held[k + 1, :, at] = earlier.astype(BF16)
+    sq_ref[...] = jnp.zeros_like(sq_ref)
+    entering = held.at[len(distances)]
+    for j in range(blocks):
+        at = pl.ds(j * wide, wide)
+        gate_block(
+            width, y_ref.at[:, at], z_ref.at[:, at], cum_ref.at[pl.ds(j, 1)], c_ref,
+            entering.at[pl.ds(0, n), at], gain_ref.at[:, at], out_ref.at[:, at], sq_ref,
+        )
 
 
 def per_device(
@@ -331,55 +387,31 @@
         name="conv_state",
     )(x_proj, x_before, conv_x, by_block(step * jnp.exp(total - cumul)), total3, b_mat)
 
-    y_local = pl.pallas_call(
-        functools.partial(local_kernel, width),
-        grid=(blocks,),
-        in_specs=[
-            full(rows), lead(rows, hb), lead(rows, hb), lead(hb, rows),
-            same(rows, n), same(rows, n), lead(1, hb),
-        ],
-        out_specs=full(rows),
-        out_shape=jax.ShapeDtypeStruct((rows, cols), F32),
-        cost_estimate=pl.CostEstimate(
-            flops=8 * rows * n * cols, bytes_accessed=8 * rows * cols, transcendentals=rows * CHUNK * heads
-        ),
-        name="local_ssd",
-    )(
-        x_conv, by_block(step), by_block(cumul), cumul.T.reshape(blocks, hb, rows),
-        b_mat, c_mat, by_block(skip[None, :]),
-    )
-    gate_proj = dot(rows_all, w_in_z)
-    fillers = [y_local, gate_proj]
-    carry = passed_along(packed, "seq", 1)
-    distance = 1
-    while distance < lax.axis_size("seq") - 1:
-        if fillers:
-            carry, done = lax.optimization_barrier((carry, fillers.pop(0)))
-            y_local, gate_proj = (done, gate_proj) if distance == 1 else (y_local, done)
-        earlier = passed_along(carry, "seq", distance).astype(F32)
-        mine = carry.astype(F32)
-        decay = mine[n : n + 1]
-        state = decay * earlier[:n] + mine[:n]
-        carry = jnp.concatenate([state, decay * earlier[n:]], axis=0).astype(BF16)
-        distance *= 2
-    entering = carry[:n]
-
+    n_seq = lax.axis_size("seq")
+    stages = 1 + max(1, (n_seq - 1).bit_length())
+    vmem = pl.BlockSpec(memory_space=pltpu.VMEM)
     gated, squares = pl.pallas_call(
-        functools.partial(gate_kernel, width),
-        grid=(blocks,),
-        in_specs=[
-            full(rows), full(rows), lead(rows, hb), same(rows, n), full(n), full(1),
-        ],
-        out_specs=[full(rows), same(rows, 1)],
+        functools.partial(chain_kernel, n_seq, width),
         out_shape=[
             jax.ShapeDtypeStruct((rows, cols), BF16),
             jax.ShapeDtypeStruct((rows, 1), F32),
         ],
-        cost_estimate=pl.CostEstimate(
-            flops=2 * rows * n * cols, bytes_accessed=10 * rows * cols, transcendentals=rows * cols
-        ),
-        name="gate",
-    )(y_local, gate_proj, by_block(jnp.exp(cumul)), c_mat, entering, norm_gain[None, :])
+        in_specs=[vmem] * 11,
+        out_specs=[vmem, vmem],
+        scratch_shapes=[
+            pltpu.VMEM((rows, cols), F32),
+            pltpu.VMEM((rows, cols), F32),
+            pltpu.VMEM((stages + 1, n + 16, cols), BF16),
+            pltpu.VMEM((stages, n + 16, cols), BF16),
+            pltpu.SemaphoreType.DMA((stages,)),
+            pltpu.SemaphoreType.DMA((stages,)),
+        ],
+        compiler_params=pltpu.CompilerParams(collective_id=2, has_side_effects=True),
+        name="state_chain",
+    )(
+        packed, rows_all, w_in_z, x_conv, by_block(step), by_block(cumul),
+        cumul.T.reshape(blocks, hb, rows), b_mat, c_mat, by_block(skip[None, :]), norm_gain[None, :],
+    )
     mixed, squares = scatter_sum(dot(gated, w_out).astype(BF16), squares[:, 0], lax.axis_size("head"))
     scale = lax.rsqrt(squares[0] / inner + 1e-05)
     return (mixed * scale[:, None]).astype(BF16)

time: 133 us -> 122 us (0.917)
  the two profiles are of different devices: /device:TPU:28 before, /device:TPU:0 now
where the time goes in v3:
time: 122 us
  Pallas kernels  91.3 us (75%)
  matrix products  12.3 us (10%)
  local copies, waits for them, and re-layouts  10.8 us (9%)
  other arithmetic  3.65 us (3%)
  starting transfers between devices  3.43 us (3%)
    pallas_call x1, Pallas kernels, per_device(): pl.pallas_call(functools.partial(chain_kernel, n_seq, width), out_shape=[...  47.8 us
    pallas_call x1, Pallas kernels, gather_tokens(): pl.pallas_call(functools.partial(gather_kernel, n), out_shape=jax.ShapeDt...  19.3 us
    pallas_call x1, Pallas kernels, scatter_sum(): pl.pallas_call(functools.partial(scatter_kernel, n), out_shape=[jax.Shape...  18.5 us
    dot_general x1, matrix products, per_device(): dot(gated, w_out).astype(BF16)  6.22 us
    pallas_call x1, Pallas kernels, per_device(): pl.pallas_call(functools.partial(conv_state_kernel, width), grid=(blocks,...  5.77 us
    reshape x6, local copies, waits for them, and re-layouts, by_block(): return a.reshape(a.shape[0], blocks, hb).transpose(1, 0, 2)  4.22 us
    ppermute x1, starting transfers between devices, passed_along(): return lax.ppermute(block, axis, route)  3.43 us
    dot_general x1, matrix products, per_device(): small = dot(rows_all, jnp.concatenate([w_in_bc, w_dt], axis=1))  3.26 us
  transfers between devices with their start and end apart: 1, of which 0 were waited for; matrix products, arithmetic and copies ran while one was open for 6% of the time, Pallas kernels for 0%

profile of v3, /device:TPU:0, one launch (start us, length us, event | category | flops | bytes accessed | tf_op | source)
XLA Modules:
  0.0 121.7 jit_solution(6814121962936161616)
XLA Ops:
  0.0 19.3 %gather_tokens.1.rows_ref = bf16[512,2048]{1,0:T(8,128)(2,1)} custom-call(bf16[128,2048]{1,0:T(8,128)(2,1)} %x_ref.1), custom_call_target="tpu_custom_call" | custom-call | tf_op jit(solution)/shard_map/gather_tokens/pallas_call | solution.py:181
  19.3 0.0 copy-done.4
  19.3 0.3 copy.30
  19.6 0.0 copy-start
  19.6 0.0 copy-start.8
  19.6 3.3 %fusion.4 = f32[512,272]{1,0:T(8,128)S(1)} fusion(bf16[512,2048]{1,0:T(8,128)(2,1)} %gather_tokens.1.rows_ref, bf16[2048,16]{1,0:T(8,128)(2,1)S(1)} %copy.30, bf16[2048,256]{1,0:T(8,128)(2,1)} %param.15), kind=kOutput, calls=%fused_computation.5 | convolution fusion | flops 572653568 | bytes 3768320 | tf_op jit(solution)/shard_map/dot_general | solution.py:347
  22.9 0.0 copy-start.2
  22.9 0.0 copy-done
  22.9 0.5 copy-done.8
  23.4 2.3 %fusion.22.x_ref = f32[512,1024]{1,0:T(8,128)S(1)} fusion(bf16[512,2048]{1,0:T(8,128)(2,1)S(1)} %copy-done, bf16[2048,1024]{1,0:T(8,128)(2,1)S(1)} %copy-done.8), kind=kOutput, calls=%fused_computation.33 | convolution fusion | flops 2147483648 | bytes 8388608 | tf_op jit(solution)/shard_map/dot_general | solution.py:346
  25.7 0.0 copy-start.1
  25.7 1.3 %copy-done.1 = f32[512,1024]{1,0:T(8,128)} copy-done((f32[512,1024]{1,0:T(8,128)}, f32[512,1024]{1,0:T(8,128)S(1)}, u32[]{:S(2)}) %copy-start.1) | copy-done | bytes 2097176
  27.1 3.4 %collective-permute-start = (f32[8,1280]{1,0:T(8,128)S(1)}, f32[8,1280]{1,0:T(8,128)S(1)}, u32[]{:S(2)}, u32[]{:S(2)}) collective-permute-start(f32[8,1280]{1,0:T(8,128)S(1)} %pad_maximum_fusion.1), channel_id=1, source_target_pairs={{0,4},{4,8},{8,12},{12,16},{16,20},{20,24},{24,28},{1,5},{5,9},{9,... | collective-permute-start | bytes 122888 | tf_op jit(solution)/shard_map/ppermute | solution.py:19
  30.5 0.0 copy-done.6
  30.5 0.2 compare_select_fusion
  30.7 0.0 copy-done.9
  30.7 0.5 fusion.7
  31.1 0.2 slice_reduce_fusion
  31.4 0.1 copy.34
  31.5 0.2 exponential_multiply_fusion
  31.7 0.0 copy-done.5
  31.7 0.0 copy-done.2
  31.7 0.0 copy-start.7
  31.7 0.0 slice-start
  31.8 0.7 transpose_reshape.3
  32.4 0.1 copy.38
  32.5 0.1 copy.35
  32.7 1.4 %copy.36 = f32[512,4,4]{2,0,1:T(8,128)} copy(f32[512,4,4]{0,2,1:T(4,128)S(1)} %reshape.27) | data formatting | bytes 65536 | tf_op jit(solution)/shard_map/reshape | solution.py:368
  34.1 1.4 %copy.40 = f32[512,4,4]{2,0,1:T(8,128)} copy(f32[512,4,4]{0,2,1:T(4,128)S(1)} %reshape.29) | data formatting | bytes 65536 | tf_op jit(solution)/shard_map/reshape | solution.py:368
  35.5 0.6 reshape.30.cumt_ref
  36.1 1.4 %copy.39 = f32[512,4,4]{2,0,1:T(8,128)} copy(f32[512,4,4]{0,2,1:T(4,128)S(1)} %reshape.28) | data formatting | bytes 65536 | tf_op jit(solution)/shard_map/reshape | solution.py:368
  37.5 0.0 copy-done.7
  37.5 0.7 transpose_reshape_broadcast_in_dim.3
  38.2 0.0 collective-permute-done
  38.2 0.0 slice-done
  38.2 0.3 multiply_convert_fusion.1
  38.5 0.7 fusion.20
  39.2 0.6 slice.71.before_ref
  39.8 5.8 %conv_state.1 = (f32[512,1024]{1,0:T(8,128)}, bf16[144,1024]{1,0:T(8,128)(2,1)}) custom-call(f32[512,1024]{1,0:T(8,128)} %copy-done.1, f32[8,1024]{1,0:T(8,128)} %slice.71.before_ref, f32[4,1024]{1,0:T(4,128)} %taps_ref.1, f32[4,512,4]{2,1,0:T(8,128)} %bitcast.27, f32[4,1,4]{2,1,0:T(1,128)} %bitcast.32, bf16[512,128]{1,0:T(8,128)(2,1)} %get-tuple-element.18.b_ref), custom_call_target="tpu_custom_call" | custom-call | flops 134217728 | bytes 4194304 | tf_op jit(solution)/shard_map/conv_state/pallas_call | solution.py:374
  45.6 47.8 %state_chain.1 = (bf16[512,1024]{1,0:T(8,128)(2,1)}, f32[512,1]{1,0:T(8,128)}) custom-call(bf16[144,1024]{1,0:T(8,128)(2,1)} %get-tuple-element.11.packed_ref, bf16[512,2048]{1,0:T(8,128)(2,1)} %gather_tokens.1.rows_ref, bf16[2048,1024]{1,0:T(8,128)(2,1)} %wz_ref.1, f32[512,1024]{1,0:T(8,128)} %get-tuple-element.12.x_ref, f32[4,512,4]{2,1,0:T(8,128)} %bitcast.29, ...), custom_call_target="tpu_custom_call" | custom-call | tf_op jit(solution)/shard_map/state_chain/pallas_call | solution.py:393
  93.4 0.0 copy-start.3
  93.4 6.2 %convolution_convert_fusion.p_ref = bf16[512,2048]{1,0:T(8,128)(2,1)} fusion(bf16[512,1024]{1,0:T(8,128)(2,1)} %get-tuple-element.13, bf16[1024,2048]{1,0:T(8,128)(2,1)} %param.23), kind=kOutput, calls=%fused_computation | convolution fusion | flops 2148532224 | bytes 7340032 | tf_op jit(solution)/shard_map/dot_general | solution.py:415
  99.6 0.0 copy-done.3
  99.6 0.1 reduce.2
  99.8 0.6 broadcast_in_dim.8.sq_ref
  100.4 18.5 %scatter_sum.1 = (f32[128,2048]{1,0:T(8,128)}, f32[8,128]{1,0:T(8,128)}) custom-call(bf16[512,2048]{1,0:T(8,128)(2,1)} %convolution_convert_fusion.p_ref, f32[4,8,128]{2,1,0:T(8,128)} %broadcast_in_dim.8.sq_ref), custom_call_target="tpu_custom_call" | custom-call | tf_op jit(solution)/shard_map/scatter_sum/pallas_call | solution.py:256
  118.9 0.7 rsqrt_bitcast_fusion
  119.5 2.1 %multiply_convert_fusion = bf16[128,2048]{1,0:T(8,128)(2,1)} fusion(f32[128,2048]{1,0:T(8,128)} %get-tuple-element.15, f32[128]{0:T(128)S(1)} %rsqrt_bitcast_fusion), kind=kLoop, calls=%fused_computation.6 | loop fusion | flops 524288 | bytes 1573376 | tf_op jit(solution)/shard_map/convert_element_type | solution.py:417
  (12 shorter events, 0.1 us)
Async XLA Ops:
  0.0 19.3 %copy-start.4 = (bf16[2048,16]{0,1:T(8,128)(2,1)S(1)}, bf16[2048,16]{0,1:T(8,128)(2,1)}, u32[]{:S(2)}) copy-start(bf16[2048,16]{0,1:T(8,128)(2,1)} %param.16) | copy-start | bytes 196612
  19.6 3.3 %copy-start = (bf16[512,2048]{1,0:T(8,128)(2,1)S(1)}, bf16[512,2048]{1,0:T(8,128)(2,1)}, u32[]{:S(2)}) copy-start(bf16[512,2048]{1,0:T(8,128)(2,1)} %gather_tokens.1.rows_ref) | copy-start | bytes 6291460
  19.6 3.8 %copy-start.8 = (bf16[2048,1024]{1,0:T(8,128)(2,1)S(1)}, bf16[2048,1024]{1,0:T(8,128)(2,1)}, u32[]{:S(2)}) copy-start(bf16[2048,1024]{1,0:T(8,128)(2,1)} %param.13) | copy-start | bytes 12582916
  22.9 8.8 %copy-start.2 = (f32[512,272]{1,0:T(8,128)}, f32[512,272]{1,0:T(8,128)S(1)}, u32[]{:S(2)}) copy-start(f32[512,272]{1,0:T(8,128)S(1)} %fusion.4) | copy-start | bytes 1671172
  23.4 7.1 %copy-start.6 = (f32[16]{0:T(128)S(1)}, f32[16]{0:T(128)}, u32[]{:S(2)}) copy-start(f32[16]{0:T(128)} %param.19) | copy-start | bytes 196
  23.4 7.3 %copy-start.9 = (f32[16]{0:T(128)S(1)}, f32[16]{0:T(128)}, u32[]{:S(2)}) copy-start(f32[16]{0:T(128)} %param.20) | copy-start | bytes 196
  25.7 1.3 %copy-start.1 = (f32[512,1024]{1,0:T(8,128)}, f32[512,1024]{1,0:T(8,128)S(1)}, u32[]{:S(2)}) copy-start(f32[512,1024]{1,0:T(8,128)S(1)} %fusion.22.x_ref) | copy-start | bytes 6291460
  27.0 4.7 %copy-start.5 = (f32[4,256]{1,0:T(4,128)S(1)}, f32[4,256]{1,0:T(4,128)}, u32[]{:S(2)}) copy-start(f32[4,256]{1,0:T(4,128)} %param.18) | copy-start | bytes 12292
  27.1 11.1 %collective-permute-start = (f32[8,1280]{1,0:T(8,128)S(1)}, f32[8,1280]{1,0:T(8,128)S(1)}, u32[]{:S(2)}, u32[]{:S(2)}) collective-permute-start(f32[8,1280]{1,0:T(8,128)S(1)} %pad_maximum_fusion.1), channel_id=1, source_target_pairs={{0,4},{4,8},{8,12},{12,16},{16,20},{20,24},{24,28},{1,5},{5,9},{9,... | collective-permute-start | bytes 122888 | tf_op jit(solution)/shard_map/ppermute | solution.py:19
  31.7 5.7 %copy-start.7 = (f32[16]{0:T(128)S(1)}, f32[16]{0:T(128)}, u32[]{:S(2)}) copy-start(f32[16]{0:T(128)} %param.21) | copy-start | bytes 196
  31.7 6.4 %slice-start = ((f32[512,272]{1,0:T(8,128)}), f32[512,256]{1,0:T(8,128)S(1)}, s32[]{:S(2)}) async-start(f32[512,272]{1,0:T(8,128)} %copy-done.2), calls=%async_computation | async-start | bytes 1048576 | tf_op jit(solution)/shard_map/slice | solution.py:348
  93.4 6.2 %copy-start.3 = (f32[512,1]{1,0:T(8,128)S(1)}, f32[512,1]{1,0:T(8,128)}, u32[]{:S(2)}) copy-start(f32[512,1]{1,0:T(8,128)} %get-tuple-element.14) | copy-start | bytes 6148

commit v4 on v3

--- a/solution.py
+++ b/solution.py
@@ -281,6 +281,8 @@
     steps = [1]
     while 2 * steps[-1] < n_seq:
         steps.append(2 * steps[-1])
+    if len(steps) == 1:
+        steps.append(2)
     barrier = pltpu.get_barrier_semaphore()
     for d in steps:
         for peer in (lax.rem(me + d, n_seq), lax.rem(me - d + n_seq, n_seq)):
@@ -301,29 +303,59 @@
         )
 
     units = [functools.partial(f, j) for j in range(blocks) for f in (local_unit, z_unit)]
-    distances = [1] + steps
-    for k, d in enumerate(distances):
-        copy = pltpu.make_async_remote_copy(
-            src_ref=packed_ref if k == 0 else held.at[k],
+    distances = [1, 2] + steps[1:]
+    last = len(distances)
+    cuts = [0] + [(k + 1) * len(units) // (last - 1) for k in range(last - 1)]
+
+    def copy_of(k, d):
+        return pltpu.make_async_remote_copy(
+            src_ref=packed_ref if k < 2 else held.at[k],
             dst_ref=came.at[k], send_sem=send_sem.at[k], recv_sem=recv_sem.at[k],
             device_id={"seq": lax.rem(me + d, n_seq)}, device_id_type=MESH,
         )
-        copy.start()
-        first = k * len(units) // len(distances)
-        for unit in units[first : (k + 1) * len(units) // len(distances)]:
+
+    def start(k):
+        d = distances[k]
+
+        @pl.when(me + d < n_seq)
+        def _():
+            copy_of(k, d).start()
+
+    def combine(k):
+        d = distances[k]
+
+        @pl.when(me >= d)
+        def _():
+            copy_of(k, d).wait_recv()
+            for j in range(blocks):
+                at = slice(j * wide, (j + 1) * wide)
+                earlier = came[k, :, at].astype(F32)
+                if k > 0:
+                    mine = held[k, :, at].astype(F32)
+                    decay = mine[n : n + 1]
+                    earlier = jnp.concatenate([decay * earlier[:n] + mine[:n], decay * earlier[n:]], axis=0)
+                held[k + 1, :, at] = earlier.astype(BF16)
+
+        @pl.when(me < d)
+        def _():
+            held[k + 1] = jnp.zeros_like(held[k + 1]) if k == 0 else held[k]
+
+        @pl.when(me + d < n_seq)
+        def _():
+            copy_of(k, d).wait_send()
+
+    start(0)
+    start(1)
+    for phase in range(last - 1):
+        for unit in units[cuts[phase] : cuts[phase + 1]]:
             unit()
-        copy.wait()
-        valid = (me >= d).astype(F32)
-        for j in range(blocks):
-            at = slice(j * wide, (j + 1) * wide)
-            earlier = came[k, :, at].astype(F32) * valid
-            if k > 0:
-                mine = held[k, :, at].astype(F32)
-                decay = mine[n : n + 1]
-                earlier = jnp.concatenate([decay * earlier[:n] + mine[:n], decay * earlier[n:]], axis=0)
-            held[k + 1, :, at] = earlier.astype(BF16)
+        if phase == 0:
+            combine(0)
+        combine(phase + 1)
+        if phase + 2 < last:
+            start(phase + 2)
     sq_ref[...] = jnp.zeros_like(sq_ref)
-    entering = held.at[len(distances)]
+    entering = held.at[last]
     for j in range(blocks):
         at = pl.ds(j * wide, wide)
         gate_block(
@@ -388,7 +420,7 @@
     )(x_proj, x_before, conv_x, by_block(step * jnp.exp(total - cumul)), total3, b_mat)
 
     n_seq = lax.axis_size("seq")
-    stages = 1 + max(1, (n_seq - 1).bit_length())
+    stages = 1 + max(2, (n_seq - 1).bit_length())
     vmem = pl.BlockSpec(memory_space=pltpu.VMEM)
     gated, squares = pl.pallas_call(
         functools.partial(chain_kernel, n_seq, width),

time: 122 us -> 117 us (0.959)
  the two profiles are of different devices: /device:TPU:0 before, /device:TPU:28 now
where the time goes in v4:
time: 117 us
  Pallas kernels  88.3 us (75%)
  matrix products  12.3 us (11%)
  local copies, waits for them, and re-layouts  10.8 us (9%)
  other arithmetic  3.65 us (3%)
  starting transfers between devices  1.29 us (1%)
    pallas_call x1, Pallas kernels, per_device(): pl.pallas_call(functools.partial(chain_kernel, n_seq, width), out_shape=[...  46.2 us
    pallas_call x1, Pallas kernels, scatter_sum(): pl.pallas_call(functools.partial(scatter_kernel, n), out_shape=[jax.Shape...  18.5 us
    pallas_call x1, Pallas kernels, gather_tokens(): pl.pallas_call(functools.partial(gather_kernel, n), out_shape=jax.ShapeDt...  17.8 us
    dot_general x1, matrix products, per_device(): dot(gated, w_out).astype(BF16)  6.22 us
    pallas_call x1, Pallas kernels, per_device(): pl.pallas_call(functools.partial(conv_state_kernel, width), grid=(blocks,...  5.77 us
    reshape x6, local copies, waits for them, and re-layouts, by_block(): return a.reshape(a.shape[0], blocks, hb).transpose(1, 0, 2)  4.22 us
    dot_general x1, matrix products, per_device(): small = dot(rows_all, jnp.concatenate([w_in_bc, w_dt], axis=1))  3.25 us
  transfers between devices with their start and end apart: 1, of which 0 were waited for; matrix products, arithmetic and copies ran while one was open for 6% of the time, Pallas kernels for 0%

profile of v4, /device:TPU:28, one launch (start us, length us, event | category | flops | bytes accessed | tf_op | source)
XLA Modules:
  0.0 116.5 jit_solution(2595084148555804919)
XLA Ops:
  0.0 17.8 %gather_tokens.1.rows_ref = bf16[512,2048]{1,0:T(8,128)(2,1)} custom-call(bf16[128,2048]{1,0:T(8,128)(2,1)} %x_ref.1), custom_call_target="tpu_custom_call" | custom-call | tf_op jit(solution)/shard_map/gather_tokens/pallas_call | solution.py:181
  17.8 0.0 copy-done.4
  17.9 0.3 copy.30
  18.1 0.0 copy-start
  18.1 0.0 copy-start.8
  18.2 3.3 %fusion.4 = f32[512,272]{1,0:T(8,128)S(1)} fusion(bf16[512,2048]{1,0:T(8,128)(2,1)} %gather_tokens.1.rows_ref, bf16[2048,16]{1,0:T(8,128)(2,1)S(1)} %copy.30, bf16[2048,256]{1,0:T(8,128)(2,1)} %param.15), kind=kOutput, calls=%fused_computation.5 | convolution fusion | flops 572653568 | bytes 3768320 | tf_op jit(solution)/shard_map/dot_general | solution.py:379
  21.4 0.0 copy-start.2
  21.4 0.0 copy-done
  21.5 0.5 copy-done.8
  21.9 2.3 %fusion.22.x_ref = f32[512,1024]{1,0:T(8,128)S(1)} fusion(bf16[512,2048]{1,0:T(8,128)(2,1)S(1)} %copy-done, bf16[2048,1024]{1,0:T(8,128)(2,1)S(1)} %copy-done.8), kind=kOutput, calls=%fused_computation.33 | convolution fusion | flops 2147483648 | bytes 8388608 | tf_op jit(solution)/shard_map/dot_general | solution.py:378
  24.2 0.0 copy-start.1
  24.3 1.3 %copy-done.1 = f32[512,1024]{1,0:T(8,128)} copy-done((f32[512,1024]{1,0:T(8,128)}, f32[512,1024]{1,0:T(8,128)S(1)}, u32[]{:S(2)}) %copy-start.1) | copy-done | bytes 2097176
  25.6 1.3 %collective-permute-start = (f32[8,1280]{1,0:T(8,128)S(1)}, f32[8,1280]{1,0:T(8,128)S(1)}, u32[]{:S(2)}, u32[]{:S(2)}) collective-permute-start(f32[8,1280]{1,0:T(8,128)S(1)} %pad_maximum_fusion.1), channel_id=1, source_target_pairs={{0,4},{4,8},{8,12},{12,16},{16,20},{20,24},{24,28},{1,5},{5,9},{9,... | collective-permute-start | bytes 122888 | tf_op jit(solution)/shard_map/ppermute | solution.py:19
  26.9 0.0 copy-done.6
  26.9 0.2 compare_select_fusion
  27.1 0.0 copy-done.9
  27.1 0.5 fusion.7
  27.5 0.2 slice_reduce_fusion
  27.8 0.1 copy.34
  27.9 0.2 exponential_multiply_fusion
  28.1 0.0 copy-done.5
  28.1 0.0 copy-done.2
  28.1 0.0 copy-start.7
  28.1 0.0 slice-start
  28.1 0.7 transpose_reshape.3
  28.8 0.1 copy.38
  28.9 0.1 copy.35
  29.1 1.4 %copy.36 = f32[512,4,4]{2,0,1:T(8,128)} copy(f32[512,4,4]{0,2,1:T(4,128)S(1)} %reshape.27) | data formatting | bytes 65536 | tf_op jit(solution)/shard_map/reshape | solution.py:400
  30.5 1.4 %copy.40 = f32[512,4,4]{2,0,1:T(8,128)} copy(f32[512,4,4]{0,2,1:T(4,128)S(1)} %reshape.29) | data formatting | bytes 65536 | tf_op jit(solution)/shard_map/reshape | solution.py:400
  31.9 0.6 reshape.30.cumt_ref
  32.5 1.4 %copy.39 = f32[512,4,4]{2,0,1:T(8,128)} copy(f32[512,4,4]{0,2,1:T(4,128)S(1)} %reshape.28) | data formatting | bytes 65536 | tf_op jit(solution)/shard_map/reshape | solution.py:400
  33.9 0.0 copy-done.7
  33.9 0.7 transpose_reshape_broadcast_in_dim.3
  34.5 0.0 collective-permute-done
  34.5 0.0 slice-done
  34.5 0.3 multiply_convert_fusion.1
  34.9 0.7 fusion.20
  35.6 0.6 slice.71.before_ref
  36.2 5.8 %conv_state.1 = (f32[512,1024]{1,0:T(8,128)}, bf16[144,1024]{1,0:T(8,128)(2,1)}) custom-call(f32[512,1024]{1,0:T(8,128)} %copy-done.1, f32[8,1024]{1,0:T(8,128)} %slice.71.before_ref, f32[4,1024]{1,0:T(4,128)} %taps_ref.1, f32[4,512,4]{2,1,0:T(8,128)} %bitcast.27, f32[4,1,4]{2,1,0:T(1,128)} %bitcast.32, bf16[512,128]{1,0:T(8,128)(2,1)} %get-tuple-element.18.b_ref), custom_call_target="tpu_custom_call" | custom-call | flops 134217728 | bytes 4194304 | tf_op jit(solution)/shard_map/conv_state/pallas_call | solution.py:406
  42.0 46.2 %state_chain.1 = (bf16[512,1024]{1,0:T(8,128)(2,1)}, f32[512,1]{1,0:T(8,128)}) custom-call(bf16[144,1024]{1,0:T(8,128)(2,1)} %get-tuple-element.11.packed_ref, bf16[512,2048]{1,0:T(8,128)(2,1)} %gather_tokens.1.rows_ref, bf16[2048,1024]{1,0:T(8,128)(2,1)} %wz_ref.1, f32[512,1024]{1,0:T(8,128)} %get-tuple-element.12.x_ref, f32[4,512,4]{2,1,0:T(8,128)} %bitcast.29, ...), custom_call_target="tpu_custom_call" | custom-call | tf_op jit(solution)/shard_map/state_chain/pallas_call | solution.py:425
  88.2 0.0 copy-start.3
  88.2 6.2 %convolution_convert_fusion.p_ref = bf16[512,2048]{1,0:T(8,128)(2,1)} fusion(bf16[512,1024]{1,0:T(8,128)(2,1)} %get-tuple-element.13, bf16[1024,2048]{1,0:T(8,128)(2,1)} %param.23), kind=kOutput, calls=%fused_computation | convolution fusion | flops 2148532224 | bytes 7340032 | tf_op jit(solution)/shard_map/dot_general | solution.py:447
  94.4 0.0 copy-done.3
  94.4 0.1 reduce.2
  94.6 0.6 broadcast_in_dim.8.sq_ref
  95.2 18.5 %scatter_sum.1 = (f32[128,2048]{1,0:T(8,128)}, f32[8,128]{1,0:T(8,128)}) custom-call(bf16[512,2048]{1,0:T(8,128)(2,1)} %convolution_convert_fusion.p_ref, f32[4,8,128]{2,1,0:T(8,128)} %broadcast_in_dim.8.sq_ref), custom_call_target="tpu_custom_call" | custom-call | tf_op jit(solution)/shard_map/scatter_sum/pallas_call | solution.py:256
  113.7 0.7 rsqrt_bitcast_fusion
  114.4 2.1 %multiply_convert_fusion = bf16[128,2048]{1,0:T(8,128)(2,1)} fusion(f32[128,2048]{1,0:T(8,128)} %get-tuple-element.15, f32[128]{0:T(128)S(1)} %rsqrt_bitcast_fusion), kind=kLoop, calls=%fused_computation.6 | loop fusion | flops 524288 | bytes 1573376 | tf_op jit(solution)/shard_map/convert_element_type | solution.py:449
  (12 shorter events, 0.1 us)
Async XLA Ops:
  0.0 17.8 %copy-start.4 = (bf16[2048,16]{0,1:T(8,128)(2,1)S(1)}, bf16[2048,16]{0,1:T(8,128)(2,1)}, u32[]{:S(2)}) copy-start(bf16[2048,16]{0,1:T(8,128)(2,1)} %param.16) | copy-start | bytes 196612
  18.1 3.3 %copy-start = (bf16[512,2048]{1,0:T(8,128)(2,1)S(1)}, bf16[512,2048]{1,0:T(8,128)(2,1)}, u32[]{:S(2)}) copy-start(bf16[512,2048]{1,0:T(8,128)(2,1)} %gather_tokens.1.rows_ref) | copy-start | bytes 6291460
  18.1 3.8 %copy-start.8 = (bf16[2048,1024]{1,0:T(8,128)(2,1)S(1)}, bf16[2048,1024]{1,0:T(8,128)(2,1)}, u32[]{:S(2)}) copy-start(bf16[2048,1024]{1,0:T(8,128)(2,1)} %param.13) | copy-start | bytes 12582916
  21.4 6.7 %copy-start.2 = (f32[512,272]{1,0:T(8,128)}, f32[512,272]{1,0:T(8,128)S(1)}, u32[]{:S(2)}) copy-start(f32[512,272]{1,0:T(8,128)S(1)} %fusion.4) | copy-start | bytes 1671172
  21.9 5.0 %copy-start.6 = (f32[16]{0:T(128)S(1)}, f32[16]{0:T(128)}, u32[]{:S(2)}) copy-start(f32[16]{0:T(128)} %param.19) | copy-start | bytes 196
  21.9 5.1 %copy-start.9 = (f32[16]{0:T(128)S(1)}, f32[16]{0:T(128)}, u32[]{:S(2)}) copy-start(f32[16]{0:T(128)} %param.20) | copy-start | bytes 196
  24.2 1.3 %copy-start.1 = (f32[512,1024]{1,0:T(8,128)}, f32[512,1024]{1,0:T(8,128)S(1)}, u32[]{:S(2)}) copy-start(f32[512,1024]{1,0:T(8,128)S(1)} %fusion.22.x_ref) | copy-start | bytes 6291460
  25.6 2.5 %copy-start.5 = (f32[4,256]{1,0:T(4,128)S(1)}, f32[4,256]{1,0:T(4,128)}, u32[]{:S(2)}) copy-start(f32[4,256]{1,0:T(4,128)} %param.18) | copy-start | bytes 12292
  25.6 9.0 %collective-permute-start = (f32[8,1280]{1,0:T(8,128)S(1)}, f32[8,1280]{1,0:T(8,128)S(1)}, u32[]{:S(2)}, u32[]{:S(2)}) collective-permute-start(f32[8,1280]{1,0:T(8,128)S(1)} %pad_maximum_fusion.1), channel_id=1, source_target_pairs={{0,4},{4,8},{8,12},{12,16},{16,20},{20,24},{24,28},{1,5},{5,9},{9,... | collective-permute-start | bytes 122888 | tf_op jit(solution)/shard_map/ppermute | solution.py:19
  28.1 5.7 %copy-start.7 = (f32[16]{0:T(128)S(1)}, f32[16]{0:T(128)}, u32[]{:S(2)}) copy-start(f32[16]{0:T(128)} %param.21) | copy-start | bytes 196
  28.1 6.4 %slice-start = ((f32[512,272]{1,0:T(8,128)}), f32[512,256]{1,0:T(8,128)S(1)}, s32[]{:S(2)}) async-start(f32[512,272]{1,0:T(8,128)} %copy-done.2), calls=%async_computation | async-start | bytes 1048576 | tf_op jit(solution)/shard_map/slice | solution.py:380
  88.2 6.2 %copy-start.3 = (f32[512,1]{1,0:T(8,128)S(1)}, f32[512,1]{1,0:T(8,128)}, u32[]{:S(2)}) copy-start(f32[512,1]{1,0:T(8,128)} %get-tuple-element.14) | copy-start | bytes 6148

commit v5 on v4

--- a/solution.py
+++ b/solution.py
@@ -109,7 +109,7 @@
 
 
 MESH = pl.DeviceIdType.MESH
-PIECES = 4
+PIECES = 8
 
 
 def greet(peers):

time: 117 us -> 117 us (level)
  no operation moved by 1% of the time
where the time goes in v5:
time: 117 us
  Pallas kernels  88.7 us (76%)
  matrix products  12.3 us (11%)
  local copies, waits for them, and re-layouts  10.8 us (9%)
  other arithmetic  3.65 us (3%)
  starting transfers between devices  1.29 us (1%)
    pallas_call x1, Pallas kernels, per_device(): pl.pallas_call(functools.partial(chain_kernel, n_seq, width), out_shape=[...  46.2 us
    pallas_call x1, Pallas kernels, scatter_sum(): pl.pallas_call(functools.partial(scatter_kernel, n), out_shape=[jax.Shape...  18.6 us
    pallas_call x1, Pallas kernels, gather_tokens(): pl.pallas_call(functools.partial(gather_kernel, n), out_shape=jax.ShapeDt...  18.1 us
    dot_general x1, matrix products, per_device(): dot(gated, w_out).astype(BF16)  6.22 us
    pallas_call x1, Pallas kernels, per_device(): pl.pallas_call(functools.partial(conv_state_kernel, width), grid=(blocks,...  5.77 us
    reshape x6, local copies, waits for them, and re-layouts, by_block(): return a.reshape(a.shape[0], blocks, hb).transpose(1, 0, 2)  4.22 us
    dot_general x1, matrix products, per_device(): small = dot(rows_all, jnp.concatenate([w_in_bc, w_dt], axis=1))  3.26 us
  transfers between devices with their start and end apart: 1, of which 0 were waited for; matrix products, arithmetic and copies ran while one was open for 6% of the time, Pallas kernels for 0%

profile of v5, /device:TPU:28, one launch (start us, length us, event | category | flops | bytes accessed | tf_op | source)
XLA Modules:
  0.0 116.9 jit_solution(6400835700329456325)
XLA Ops:
  0.0 18.1 %gather_tokens.1.rows_ref = bf16[512,2048]{1,0:T(8,128)(2,1)} custom-call(bf16[128,2048]{1,0:T(8,128)(2,1)} %x_ref.1), custom_call_target="tpu_custom_call" | custom-call | tf_op jit(solution)/shard_map/gather_tokens/pallas_call | solution.py:181
  18.1 0.0 copy-done.4
  18.1 0.3 copy.30
  18.4 0.0 copy-start
  18.4 0.0 copy-start.8
  18.4 3.3 %fusion.4 = f32[512,272]{1,0:T(8,128)S(1)} fusion(bf16[512,2048]{1,0:T(8,128)(2,1)} %gather_tokens.1.rows_ref, bf16[2048,16]{1,0:T(8,128)(2,1)S(1)} %copy.30, bf16[2048,256]{1,0:T(8,128)(2,1)} %param.15), kind=kOutput, calls=%fused_computation.5 | convolution fusion | flops 572653568 | bytes 3768320 | tf_op jit(solution)/shard_map/dot_general | solution.py:379
  21.7 0.0 copy-start.2
  21.7 0.0 copy-done
  21.7 0.5 copy-done.8
  22.2 2.3 %fusion.22.x_ref = f32[512,1024]{1,0:T(8,128)S(1)} fusion(bf16[512,2048]{1,0:T(8,128)(2,1)S(1)} %copy-done, bf16[2048,1024]{1,0:T(8,128)(2,1)S(1)} %copy-done.8), kind=kOutput, calls=%fused_computation.33 | convolution fusion | flops 2147483648 | bytes 8388608 | tf_op jit(solution)/shard_map/dot_general | solution.py:378
  24.5 0.0 copy-start.1
  24.5 1.3 %copy-done.1 = f32[512,1024]{1,0:T(8,128)} copy-done((f32[512,1024]{1,0:T(8,128)}, f32[512,1024]{1,0:T(8,128)S(1)}, u32[]{:S(2)}) %copy-start.1) | copy-done | bytes 2097176
  25.9 1.3 %collective-permute-start = (f32[8,1280]{1,0:T(8,128)S(1)}, f32[8,1280]{1,0:T(8,128)S(1)}, u32[]{:S(2)}, u32[]{:S(2)}) collective-permute-start(f32[8,1280]{1,0:T(8,128)S(1)} %pad_maximum_fusion.1), channel_id=1, source_target_pairs={{0,4},{4,8},{8,12},{12,16},{16,20},{20,24},{24,28},{1,5},{5,9},{9,... | collective-permute-start | bytes 122888 | tf_op jit(solution)/shard_map/ppermute | solution.py:19
  27.2 0.0 copy-done.6
  27.2 0.2 compare_select_fusion
  27.3 0.0 copy-done.9
  27.3 0.5 fusion.7
  27.8 0.2 slice_reduce_fusion
  28.0 0.1 copy.34
  28.2 0.2 exponential_multiply_fusion
  28.4 0.0 copy-done.5
  28.4 0.0 copy-done.2
  28.4 0.0 copy-start.7
  28.4 0.0 slice-start
  28.4 0.7 transpose_reshape.3
  29.1 0.1 copy.38
  29.2 0.1 copy.35
  29.3 1.4 %copy.36 = f32[512,4,4]{2,0,1:T(8,128)} copy(f32[512,4,4]{0,2,1:T(4,128)S(1)} %reshape.27) | data formatting | bytes 65536 | tf_op jit(solution)/shard_map/reshape | solution.py:400
  30.8 1.4 %copy.40 = f32[512,4,4]{2,0,1:T(8,128)} copy(f32[512,4,4]{0,2,1:T(4,128)S(1)} %reshape.29) | data formatting | bytes 65536 | tf_op jit(solution)/shard_map/reshape | solution.py:400
  32.2 0.6 reshape.30.cumt_ref
  32.8 1.4 %copy.39 = f32[512,4,4]{2,0,1:T(8,128)} copy(f32[512,4,4]{0,2,1:T(4,128)S(1)} %reshape.28) | data formatting | bytes 65536 | tf_op jit(solution)/shard_map/reshape | solution.py:400
  34.1 0.0 copy-done.7
  34.1 0.7 transpose_reshape_broadcast_in_dim.3
  34.8 0.0 collective-permute-done
  34.8 0.0 slice-done
  34.8 0.3 multiply_convert_fusion.1
  35.2 0.7 fusion.20
  35.9 0.6 slice.71.before_ref
  36.5 5.8 %conv_state.1 = (f32[512,1024]{1,0:T(8,128)}, bf16[144,1024]{1,0:T(8,128)(2,1)}) custom-call(f32[512,1024]{1,0:T(8,128)} %copy-done.1, f32[8,1024]{1,0:T(8,128)} %slice.71.before_ref, f32[4,1024]{1,0:T(4,128)} %taps_ref.1, f32[4,512,4]{2,1,0:T(8,128)} %bitcast.27, f32[4,1,4]{2,1,0:T(1,128)} %bitcast.32, bf16[512,128]{1,0:T(8,128)(2,1)} %get-tuple-element.18.b_ref), custom_call_target="tpu_custom_call" | custom-call | flops 134217728 | bytes 4194304 | tf_op jit(solution)/shard_map/conv_state/pallas_call | solution.py:406
  42.3 46.2 %state_chain.1 = (bf16[512,1024]{1,0:T(8,128)(2,1)}, f32[512,1]{1,0:T(8,128)}) custom-call(bf16[144,1024]{1,0:T(8,128)(2,1)} %get-tuple-element.11.packed_ref, bf16[512,2048]{1,0:T(8,128)(2,1)} %gather_tokens.1.rows_ref, bf16[2048,1024]{1,0:T(8,128)(2,1)} %wz_ref.1, f32[512,1024]{1,0:T(8,128)} %get-tuple-element.12.x_ref, f32[4,512,4]{2,1,0:T(8,128)} %bitcast.29, ...), custom_call_target="tpu_custom_call" | custom-call | tf_op jit(solution)/shard_map/state_chain/pallas_call | solution.py:425
  88.5 0.0 copy-start.3
  88.5 6.2 %convolution_convert_fusion.p_ref = bf16[512,2048]{1,0:T(8,128)(2,1)} fusion(bf16[512,1024]{1,0:T(8,128)(2,1)} %get-tuple-element.13, bf16[1024,2048]{1,0:T(8,128)(2,1)} %param.23), kind=kOutput, calls=%fused_computation | convolution fusion | flops 2148532224 | bytes 7340032 | tf_op jit(solution)/shard_map/dot_general | solution.py:447
  94.7 0.0 copy-done.3
  94.7 0.1 reduce.2
  94.8 0.6 broadcast_in_dim.8.sq_ref
  95.4 18.6 %scatter_sum.1 = (f32[128,2048]{1,0:T(8,128)}, f32[8,128]{1,0:T(8,128)}) custom-call(bf16[512,2048]{1,0:T(8,128)(2,1)} %convolution_convert_fusion.p_ref, f32[4,8,128]{2,1,0:T(8,128)} %broadcast_in_dim.8.sq_ref), custom_call_target="tpu_custom_call" | custom-call | tf_op jit(solution)/shard_map/scatter_sum/pallas_call | solution.py:256
  114.1 0.7 rsqrt_bitcast_fusion
  114.8 2.1 %multiply_convert_fusion = bf16[128,2048]{1,0:T(8,128)(2,1)} fusion(f32[128,2048]{1,0:T(8,128)} %get-tuple-element.15, f32[128]{0:T(128)S(1)} %rsqrt_bitcast_fusion), kind=kLoop, calls=%fused_computation.6 | loop fusion | flops 524288 | bytes 1573376 | tf_op jit(solution)/shard_map/convert_element_type | solution.py:449
  (12 shorter events, 0.1 us)
Async XLA Ops:
  0.0 18.1 %copy-start.4 = (bf16[2048,16]{0,1:T(8,128)(2,1)S(1)}, bf16[2048,16]{0,1:T(8,128)(2,1)}, u32[]{:S(2)}) copy-start(bf16[2048,16]{0,1:T(8,128)(2,1)} %param.16) | copy-start | bytes 196612
  18.4 3.3 %copy-start = (bf16[512,2048]{1,0:T(8,128)(2,1)S(1)}, bf16[512,2048]{1,0:T(8,128)(2,1)}, u32[]{:S(2)}) copy-start(bf16[512,2048]{1,0:T(8,128)(2,1)} %gather_tokens.1.rows_ref) | copy-start | bytes 6291460
  18.4 3.8 %copy-start.8 = (bf16[2048,1024]{1,0:T(8,128)(2,1)S(1)}, bf16[2048,1024]{1,0:T(8,128)(2,1)}, u32[]{:S(2)}) copy-start(bf16[2048,1024]{1,0:T(8,128)(2,1)} %param.13) | copy-start | bytes 12582916
  21.7 6.7 %copy-start.2 = (f32[512,272]{1,0:T(8,128)}, f32[512,272]{1,0:T(8,128)S(1)}, u32[]{:S(2)}) copy-start(f32[512,272]{1,0:T(8,128)S(1)} %fusion.4) | copy-start | bytes 1671172
  22.2 5.0 %copy-start.6 = (f32[16]{0:T(128)S(1)}, f32[16]{0:T(128)}, u32[]{:S(2)}) copy-start(f32[16]{0:T(128)} %param.19) | copy-start | bytes 196
  22.2 5.1 %copy-start.9 = (f32[16]{0:T(128)S(1)}, f32[16]{0:T(128)}, u32[]{:S(2)}) copy-start(f32[16]{0:T(128)} %param.20) | copy-start | bytes 196
  24.5 1.3 %copy-start.1 = (f32[512,1024]{1,0:T(8,128)}, f32[512,1024]{1,0:T(8,128)S(1)}, u32[]{:S(2)}) copy-start(f32[512,1024]{1,0:T(8,128)S(1)} %fusion.22.x_ref) | copy-start | bytes 6291460
  25.8 2.5 %copy-start.5 = (f32[4,256]{1,0:T(4,128)S(1)}, f32[4,256]{1,0:T(4,128)}, u32[]{:S(2)}) copy-start(f32[4,256]{1,0:T(4,128)} %param.18) | copy-start | bytes 12292
  25.9 9.0 %collective-permute-start = (f32[8,1280]{1,0:T(8,128)S(1)}, f32[8,1280]{1,0:T(8,128)S(1)}, u32[]{:S(2)}, u32[]{:S(2)}) collective-permute-start(f32[8,1280]{1,0:T(8,128)S(1)} %pad_maximum_fusion.1), channel_id=1, source_target_pairs={{0,4},{4,8},{8,12},{12,16},{16,20},{20,24},{24,28},{1,5},{5,9},{9,... | collective-permute-start | bytes 122888 | tf_op jit(solution)/shard_map/ppermute | solution.py:19
  28.4 5.7 %copy-start.7 = (f32[16]{0:T(128)S(1)}, f32[16]{0:T(128)}, u32[]{:S(2)}) copy-start(f32[16]{0:T(128)} %param.21) | copy-start | bytes 196
  28.4 6.4 %slice-start = ((f32[512,272]{1,0:T(8,128)}), f32[512,256]{1,0:T(8,128)S(1)}, s32[]{:S(2)}) async-start(f32[512,272]{1,0:T(8,128)} %copy-done.2), calls=%async_computation | async-start | bytes 1048576 | tf_op jit(solution)/shard_map/slice | solution.py:380
  88.5 6.2 %copy-start.3 = (f32[512,1]{1,0:T(8,128)S(1)}, f32[512,1]{1,0:T(8,128)}, u32[]{:S(2)}) copy-start(f32[512,1]{1,0:T(8,128)} %get-tuple-element.14) | copy-start | bytes 6148
